TPU v7x, 128 devices: a whole 4x4x4 slice. The times are simulated.
128 devices in a mesh: row: 16 (over y, z), col: 8 (over x, core).
Axes of the slice: x: 4, y: 4, z: 4, core: 2. Of those that a mesh axis runs over, the one named last changes fastest.
Arguments:
- feats: bfloat16 [64, 32, 128, 512], P('row', 'col'), may hold values from -20 to 20
- virt_emb: bfloat16 [4, 512], replicated, may hold values from -18 to 18
- w_query: bfloat16 [512, 512], replicated, may hold values from -1 to 1
- w_key: bfloat16 [512, 512], replicated, may hold values from -1 to 1
- w_value: bfloat16 [512, 512], replicated, may hold values from -0.25 to 0.25
- w_out: bfloat16 [512, 512], replicated, may hold values from -0.25 to 0.25
- link_mask: int32 [64, 32, 4], P('row', 'col'), may hold values 0 or 1
- partners: int32 [64, 32, 4], P('row', 'col'), may hold values from 0 to 2047, as said below
- virt_ids: int32 [64, 32, 128], P('row', 'col'), may hold values from 0 to 3
Outputs:
- node_out: bfloat16 [64, 32, 128, 512], P('row', 'col')
- virt_out: float32 [4, 512], replicated
Inputs may be any that keep to these rules, and one draw needn't show every extreme that they name: For every m, partners[., ., m] is a perfect matching of the blocks: the partner of a block lies on another device, and the partner's entry for m names the block back. Counted over all 4 matchings, the blocks of one device have at most 1 partners on any one device, and exactly 1 on some device.
All inputs are finite; a program needn't handle non-finite values. No bound on the sum of `link_mask` on one device may be relied on, other than what follows from the above.
Results may differ from a plain program's by a relative error of at most 0.0077.
Values may be sent and summed in bfloat16 or wider, within the bound.
A program may use at most 192 MiB of HBM per device.

v0:
```python
import math

import jax
import jax.numpy as jnp
from jax import lax
from jax.sharding import PartitionSpec as P

D = 512
H = 8
HD = 64
BLK = 128
NEXP = 4
NVIRT = 4


NEG_FILL = -1e30
GROUP_BLOCKS = 4


def extended(block, sides, width):
    for axis, dim in sides:
        count = lax.axis_size(axis)
        forward = [(i, i + 1) for i in range(count - 1)]
        backward = [(target, source) for source, target in forward]
        low = lax.ppermute(
            lax.slice_in_dim(block, block.shape[dim] - width, None, axis=dim), axis, forward
        )
        high = lax.ppermute(lax.slice_in_dim(block, 0, width, axis=dim), axis, backward)
        block = jnp.concatenate([low, block, high], axis=dim)
    return block


def weigh_members(scores, membership, top, values_grouped):
    shares = jnp.where(membership, jnp.exp(scores - top[..., None]), 0.0)
    group_count = values_grouped.shape[0]
    shares_grouped = jnp.transpose(
        shares.reshape(shares.shape[0], shares.shape[1], group_count, -1), (2, 0, 1, 3)
    )

    def one_group(pair):
        return jnp.einsum(
            "vhn,nhd->vhd", pair[0], pair[1].astype(jnp.float32), precision=lax.Precision.HIGHEST
        )

    partial_sums = lax.map(one_group, (shares_grouped, values_grouped))
    return (jnp.sum(shares, axis=-1), jnp.sum(partial_sums, axis=0))


def shards(feats, virt_emb, w_query, w_key, w_value, w_out, link_mask, partners, virt_ids):
    blocks_x, blocks_y = (feats.shape[0], feats.shape[1])
    nblocks = blocks_x * blocks_y
    rows_total = nblocks * BLK
    scale = 1.0 / math.sqrt(HD)
    flat = feats.reshape(rows_total, D)
    w_pair = jnp.concatenate([w_key, w_value], axis=1)
    queries = jnp.dot(flat, w_query, preferred_element_type=jnp.float32).astype(jnp.bfloat16)
    key_value = jnp.dot(flat, w_pair, preferred_element_type=jnp.float32).astype(jnp.bfloat16)
    virtual_query = (
        jnp.dot(virt_emb, w_query, preferred_element_type=jnp.float32)
        .astype(jnp.bfloat16)
        .reshape(NVIRT, H, HD)
    )
    virtual_pair = jnp.dot(virt_emb, w_pair, preferred_element_type=jnp.float32).astype(
        jnp.bfloat16
    )
    virtual_keys = virtual_pair[:, :D].reshape(NVIRT, H, HD)
    virtual_values = virtual_pair[:, D:].reshape(NVIRT, H, HD)
    padded = extended(
        key_value.reshape(blocks_x, blocks_y, BLK, 2 * D), (("row", 0), ("col", 1)), 1
    )
    padded_flat = padded.reshape((blocks_x + 2) * (blocks_y + 2), BLK, 2 * D)
    mesh_rows = lax.axis_size("row")
    mesh_cols = lax.axis_size("col")
    devices = mesh_rows * mesh_cols
    slot_count = nblocks * NEXP
    capacity = (slot_count + devices - 2) // (devices - 1)
    grid_cols = blocks_y * mesh_cols
    partner_ids = jnp.transpose(partners, (2, 0, 1)).reshape(slot_count)
    partner_row = partner_ids // grid_cols
    partner_col = partner_ids % grid_cols
    dest = partner_row // blocks_x * mesh_cols + partner_col // blocks_y
    partner_slot = partner_row % blocks_x * blocks_y + partner_col % blocks_y
    order = jnp.arange(slot_count, dtype=jnp.int32)
    own_slot = order % nblocks
    recv_order = order // nblocks * nblocks + partner_slot
    same_dest = dest[:, None] == dest[None, :]
    rank_out = jnp.sum(same_dest & (order[None, :] < order[:, None]), axis=1)
    rank_in = jnp.sum(same_dest & (recv_order[None, :] < recv_order[:, None]), axis=1)
    target = dest * capacity + rank_out
    hits = target[None, :] == jnp.arange(devices * capacity, dtype=jnp.int32)[:, None]
    source_block = jnp.sum(jnp.where(hits, own_slot[None, :], 0), axis=1)
    filled = jnp.any(hits, axis=1)
    sendable = feats.reshape(nblocks, BLK, D)
    lane_width = sendable.shape[2]
    outgoing = jnp.where(
        filled[:, None, None], jnp.take(sendable, source_block, axis=0), jnp.zeros((), jnp.bfloat16)
    )
    arrived = lax.all_to_all(
        outgoing.reshape(devices, capacity, BLK, lane_width),
        ("row", "col"),
        split_axis=0,
        concat_axis=0,
        tiled=True,
    )
    arrived = arrived.reshape(devices * capacity, BLK, lane_width)
    picked = jnp.take(arrived, dest * capacity + rank_in, axis=0)
    remote = (
        jnp.dot(picked.reshape(slot_count * BLK, D), w_pair, preferred_element_type=jnp.float32)
        .astype(jnp.bfloat16)
        .reshape(NEXP, nblocks, BLK, 2 * D)
    )
    grid_rows = mesh_rows * blocks_x
    block_ids = jnp.arange(nblocks, dtype=jnp.int32)
    global_row = lax.axis_index("row") * blocks_x + block_ids // blocks_y
    global_col = lax.axis_index("col") * blocks_y + block_ids % blocks_y
    links = link_mask.reshape(nblocks, 4) == 1
    always = jnp.ones((nblocks,), bool)
    live_table = jnp.stack(
        [
            always,
            links[:, 0] & (global_row > 0),
            links[:, 1] & (global_row < grid_rows - 1),
            links[:, 2] & (global_col > 0),
            links[:, 3] & (global_col < grid_cols - 1),
        ]
        + [always] * NEXP,
        axis=1,
    )
    query_blocks = queries.reshape(nblocks, BLK, H, HD)
    id_blocks = virt_ids.reshape(nblocks, BLK)
    virtual_slots = jnp.arange(NVIRT, dtype=jnp.int32)
    stride = blocks_y + 2
    offsets = jnp.array([0, -stride, stride, -1, 1], jnp.int32)
    key_count = (5 + NEXP) * BLK
    group_count = nblocks // GROUP_BLOCKS

    def attend(group):
        first = group * GROUP_BLOCKS
        in_group = first + jnp.arange(GROUP_BLOCKS, dtype=jnp.int32)
        centre = (in_group // blocks_y + 1) * stride + in_group % blocks_y + 1
        nearby = jnp.take(
            padded_flat, (centre[:, None] + offsets[None, :]).reshape(-1), axis=0
        ).reshape(GROUP_BLOCKS, 5, BLK, 2 * D)
        distant = jnp.transpose(
            lax.dynamic_slice_in_dim(remote, first, GROUP_BLOCKS, 1), (1, 0, 2, 3)
        )
        gathered = jnp.concatenate([nearby, distant], axis=1)
        group_keys = gathered[..., :D].reshape(GROUP_BLOCKS, key_count, H, HD)
        group_values = gathered[..., D:].reshape(GROUP_BLOCKS, key_count, H, HD)
        group_query = lax.dynamic_slice_in_dim(query_blocks, first, GROUP_BLOCKS, 0)
        live = jnp.repeat(lax.dynamic_slice_in_dim(live_table, first, GROUP_BLOCKS, 0), BLK, axis=1)
        scores = (
            jnp.einsum(
                "bqhd,bkhd->bhqk", group_query, group_keys, preferred_element_type=jnp.float32
            )
            * scale
        )
        scores = jnp.where(live[:, None, None, :], scores, NEG_FILL)
        chosen = (
            lax.dynamic_slice_in_dim(id_blocks, first, GROUP_BLOCKS, 0)[:, None, :, None]
            == virtual_slots
        )
        virtual_all = (
            jnp.einsum(
                "bqhd,vhd->bhqv", group_query, virtual_keys, preferred_element_type=jnp.float32
            )
            * scale
        )
        virtual_score = jnp.sum(jnp.where(chosen, virtual_all, 0.0), axis=-1)
        top = jnp.maximum(jnp.max(scores, axis=-1), virtual_score)
        shares = jnp.exp(scores - top[..., None])
        virtual_share = jnp.exp(virtual_score - top)
        total = jnp.sum(shares, axis=-1) + virtual_share
        weights = (shares / total[..., None]).astype(jnp.bfloat16)
        virtual_weight = (virtual_share / total).astype(jnp.bfloat16)
        picked_weight = jnp.where(chosen, virtual_weight[..., None], jnp.zeros((), jnp.bfloat16))
        context = jnp.einsum(
            "bhqk,bkhd->bqhd", weights, group_values, preferred_element_type=jnp.float32
        )
        context = context + jnp.einsum(
            "bhqv,vhd->bqhd", picked_weight, virtual_values, preferred_element_type=jnp.float32
        )
        return context.astype(jnp.bfloat16)

    contexts = lax.map(attend, jnp.arange(group_count, dtype=jnp.int32))
    mixed = flat.astype(jnp.float32) + jnp.dot(
        contexts.reshape(rows_total, D), w_out, preferred_element_type=jnp.float32
    )
    node_out = mixed.astype(jnp.bfloat16).reshape(blocks_x, blocks_y, BLK, D)
    node_keys = key_value[:, :D].reshape(rows_total, H, HD)
    values_grouped = key_value[:, D:].reshape(group_count, GROUP_BLOCKS * BLK, H, HD)
    virtual_scores = (
        jnp.einsum("vhd,nhd->vhn", virtual_query, node_keys, preferred_element_type=jnp.float32)
        * scale
    )
    membership = virt_ids.reshape(1, 1, rows_total) == virtual_slots[:, None, None]
    virtual_scores = jnp.where(membership, virtual_scores, NEG_FILL)
    own_score = (
        jnp.sum(virtual_query.astype(jnp.float32) * virtual_keys.astype(jnp.float32), axis=-1)
        * scale
    )
    local_top = jnp.max(virtual_scores, axis=-1)
    top = jnp.maximum(lax.pmax(local_top, ("row", "col")), own_score)
    local_total, local_accum = weigh_members(virtual_scores, membership, top, values_grouped)
    total, accum = lax.psum((local_total, local_accum), ("row", "col"))
    final_top = jnp.maximum(top, own_score)
    rescale = jnp.exp(top - final_top)
    own_share = jnp.exp(own_score - final_top)
    total = total * rescale + own_share
    accum = accum * rescale[..., None] + own_share[..., None] * virtual_values.astype(jnp.float32)
    virtual_context = (accum / total[..., None]).astype(jnp.bfloat16).reshape(NVIRT, D)
    virt_out = virt_emb.astype(jnp.float32) + jnp.dot(
        virtual_context, w_out, preferred_element_type=jnp.float32
    )
    return (node_out, virt_out)


def solution(mesh):
    return jax.shard_map(
        shards,
        mesh=mesh,
        in_specs=(
            P("row", "col", None, None),
            P(),
            P(),
            P(),
            P(),
            P(),
            P("row", "col", None),
            P("row", "col", None),
            P("row", "col", None),
        ),
        out_specs=(P("row", "col", None, None), P()),
        check_vma=False,
    )
```

profile of v0, /device:TPU:1, one launch (start us, length us, event | category | flops | bytes accessed | tf_op | source)
XLA Modules:
  0.0 923.1 jit_solution(12527950100700657730)
XLA Ops:
  11.8 14.4 %fusion.29 = bf16[128,1,128,512]{3,2,1,0:T(8,128)(2,1)} fusion(bf16[128,128,512]{2,1,0:T(8,128)(2,1)} %gather_fusion.1, pred[128]{0:T(512)(128)(4,1)S(1)} %compare_and_fusion.7, pred[128]{0:T(512)(128)(4,1)S(1)} %fusion.33), kind=kLoop, calls=%fused_computation.64 | loop fusion | flops 16777216 | bytes 33554688 | tf_op jit(solution)/shard_map/jit(_where)/select_n | solution.py:95
  26.2 11.9 %all-to-all-start = ((bf16[128,1,128,512]{3,2,1,0:T(8,128)(2,1)}), bf16[128,1,128,512]{3,2,1,0:T(8,128)(2,1)}, u32[]{:S(2)}, u32[]{:S(2)}) async-start(bf16[128,1,128,512]{3,2,1,0:T(8,128)(2,1)} %fusion.29), calls=%async_computation | async-start | bytes 33554432 | tf_op jit(solution)/shard_map/all_to_all | solution.py:98
  60.9 277.3 %pmax.7 = f32[4,8]{0,1:T(8,128)S(1)} all-reduce(f32[4,8]{0,1:T(8,128)S(1)} %get-tuple-element.401), channel_id=1, replica_groups=mesh['row'=16,'col'=8] {'row','col'}, use_global_device_ids=true, to_apply=%region_10.11 | all-reduce | flops 32 | bytes 256 | tf_op jit(solution)/shard_map/pmax | solution.py:203
  382.3 66.1 %all-reduce = (f32[4,8,64]{2,0,1:T(4,128)S(1)}, f32[4,8]{0,1:T(8,128)S(1)}) all-reduce(f32[4,8,64]{2,0,1:T(4,128)S(1)} %reduce_sum.92, f32[4,8]{0,1:T(8,128)S(1)} %get-tuple-element.377), channel_id=1, replica_groups=mesh['row'=16,'col'=8] {'row','col'}, use_global_device_ids=true, to_apply=%region_15.16 | all-reduce | flops 2080 | bytes 16640 | tf_op jit(solution)/shard_map/psum | solution.py:205
  457.5 11.3 %gather_fusion.2 = bf16[64,128,512]{2,1,0:T(8,128)(2,1)} fusion(bf16[128,128,512]{2,1,0:T(8,128)(2,1)} %bitcast.16, s32[1024]{0:T(1024)S(1)} %pad_clamp_fusion.1), kind=kCustom, calls=%fused_computation.2 | custom fusion | bytes 16777472 | tf_op jit(solution)/shard_map/jit(_take)/gather | solution.py:106
  473.6 11.6 %convolution_convert_fusion = bf16[8192,1024]{1,0:T(8,128)(2,1)} fusion(bf16[8192,512]{1,0:T(8,128)(2,1)S(1)} %bitcast_select_fusion.1, bf16[512,1024]{1,0:T(8,128)(2,1)S(1)} %copy-done.8), kind=kOutput, calls=%fused_computation.65 | convolution fusion | flops 8598323200 | bytes 26214400 | tf_op jit(solution)/shard_map/dot_general | solution.py:108
  485.3 430.2 %while.26 = (s32[]{:T(128)}, bf16[4,4,128,8,64]{2,1,0,4,3:T(4,128)(2,1)}, s32[4]{0:T(128)S(1)}, bf16[36,128,1024]{2,1,0:T(8,128)(2,1)}, bf16[4,16,128,1024]{3,2,...) while((s32[]{:T(128)}, ...), condition=%wide.region_8.9_spmd.clone.clone, body=%wide.region_4.8_spmd.sunk.clone.clone.sunk | while | flops 1272003840 | bytes 190594160 | solution.py:185
  507.4 11.6 %copy.223 = bf16[4,5,128,1024]{2,1,3,0:T(8,128)(2,1)} copy(bf16[4,5,128,1024]{3,2,1,0:T(8,128)(2,1)} %bitcast.168) | data formatting | bytes 10485760 | tf_op jit(solution)/shard_map/while/body/eval_jaxpr/jit(_take)/gather | solution.py:141
  527.0 11.9 %pad_maximum_fusion.6 = (bf16[4,9,128,512]{2,1,3,0:T(8,128)(2,1)}, bf16[4,9,128,512]{2,1,3,0:T(8,128)(2,1)}) fusion(bf16[4,4,128,1024]{2,1,3,0:T(4,128)(2,1)S(1)} %bitcast.169, bf16[4,5,128,1024]{2,1,3,0:T(8,128)(2,1)} %broadcast_select_fusion.2), kind=kLoop, calls=%fused_computation.19.clone.1 | loop fusion | flops 18874368 | bytes 18874368 | tf_op jit(solution)/shard_map/while/body/eval_jaxpr/concatenate | solution.py:147
  549.6 10.9 %reshape.845 = bf16[4,1152,8,64]{1,3,2,0:T(8,128)(2,1)} reshape(bf16[4,9,128,512]{2,1,3,0:T(8,128)(2,1)} %get-tuple-element.500) | data formatting | bytes 9437184 | tf_op jit(solution)/shard_map/while/body/eval_jaxpr/reshape | solution.py:148
  560.5 11.5 %fusion.98 = (f32[4,8,128]{2,1,0:T(8,128)S(1)}, f32[4,8,128,1152]{3,2,1,0:T(8,128)}) fusion(bf16[4,1152,8,64]{1,3,2,0:T(8,128)(2,1)} %reshape.845, pred[4,1152]{1,0:T(4,128)(4,1)S(1)} %bitcast.178, bf16[16,128,8,64]{1,3,2,0:T(8,128)(2,1)S(1)} %copy-done.6, s32[]{:T(128)S(6)} %select_n.523), kind=kOutput, calls=%fused_computation.165.clone.1 | convolution fusion | flops 618131456 | bytes 24138244 | tf_op jit(solution)/shard_map/while/body/eval_jaxpr/bqhd,bkhd->bhqk/dot_general | solution.py:153
  615.0 11.6 %copy.223 = bf16[4,5,128,1024]{2,1,3,0:T(8,128)(2,1)} copy(bf16[4,5,128,1024]{3,2,1,0:T(8,128)(2,1)} %bitcast.168) | data formatting | bytes 10485760 | tf_op jit(solution)/shard_map/while/body/eval_jaxpr/jit(_take)/gather | solution.py:141
  634.5 11.9 %pad_maximum_fusion.6 = (bf16[4,9,128,512]{2,1,3,0:T(8,128)(2,1)}, bf16[4,9,128,512]{2,1,3,0:T(8,128)(2,1)}) fusion(bf16[4,4,128,1024]{2,1,3,0:T(4,128)(2,1)S(1)} %bitcast.169, bf16[4,5,128,1024]{2,1,3,0:T(8,128)(2,1)} %broadcast_select_fusion.2), kind=kLoop, calls=%fused_computation.19.clone.1 | loop fusion | flops 18874368 | bytes 18874368 | tf_op jit(solution)/shard_map/while/body/eval_jaxpr/concatenate | solution.py:147
  646.4 10.8 %reshape.844 = bf16[4,1152,8,64]{1,3,2,0:T(8,128)(2,1)} reshape(bf16[4,9,128,512]{2,1,3,0:T(8,128)(2,1)} %get-tuple-element.499) | data formatting | bytes 9437184 | tf_op jit(solution)/shard_map/while/body/eval_jaxpr/reshape | solution.py:149
  657.2 10.9 %reshape.845 = bf16[4,1152,8,64]{1,3,2,0:T(8,128)(2,1)} reshape(bf16[4,9,128,512]{2,1,3,0:T(8,128)(2,1)} %get-tuple-element.500) | data formatting | bytes 9437184 | tf_op jit(solution)/shard_map/while/body/eval_jaxpr/reshape | solution.py:148
  668.1 11.5 %fusion.98 = (f32[4,8,128]{2,1,0:T(8,128)S(1)}, f32[4,8,128,1152]{3,2,1,0:T(8,128)}) fusion(bf16[4,1152,8,64]{1,3,2,0:T(8,128)(2,1)} %reshape.845, pred[4,1152]{1,0:T(4,128)(4,1)S(1)} %bitcast.178, bf16[16,128,8,64]{1,3,2,0:T(8,128)(2,1)S(1)} %copy-done.6, s32[]{:T(128)S(6)} %select_n.523), kind=kOutput, calls=%fused_computation.165.clone.1 | convolution fusion | flops 618131456 | bytes 24138244 | tf_op jit(solution)/shard_map/while/body/eval_jaxpr/bqhd,bkhd->bhqk/dot_general | solution.py:153
  722.6 11.6 %copy.223 = bf16[4,5,128,1024]{2,1,3,0:T(8,128)(2,1)} copy(bf16[4,5,128,1024]{3,2,1,0:T(8,128)(2,1)} %bitcast.168) | data formatting | bytes 10485760 | tf_op jit(solution)/shard_map/while/body/eval_jaxpr/jit(_take)/gather | solution.py:141
  742.1 11.9 %pad_maximum_fusion.6 = (bf16[4,9,128,512]{2,1,3,0:T(8,128)(2,1)}, bf16[4,9,128,512]{2,1,3,0:T(8,128)(2,1)}) fusion(bf16[4,4,128,1024]{2,1,3,0:T(4,128)(2,1)S(1)} %bitcast.169, bf16[4,5,128,1024]{2,1,3,0:T(8,128)(2,1)} %broadcast_select_fusion.2), kind=kLoop, calls=%fused_computation.19.clone.1 | loop fusion | flops 18874368 | bytes 18874368 | tf_op jit(solution)/shard_map/while/body/eval_jaxpr/concatenate | solution.py:147
  764.7 10.9 %reshape.845 = bf16[4,1152,8,64]{1,3,2,0:T(8,128)(2,1)} reshape(bf16[4,9,128,512]{2,1,3,0:T(8,128)(2,1)} %get-tuple-element.500) | data formatting | bytes 9437184 | tf_op jit(solution)/shard_map/while/body/eval_jaxpr/reshape | solution.py:148
  775.7 11.5 %fusion.98 = (f32[4,8,128]{2,1,0:T(8,128)S(1)}, f32[4,8,128,1152]{3,2,1,0:T(8,128)}) fusion(bf16[4,1152,8,64]{1,3,2,0:T(8,128)(2,1)} %reshape.845, pred[4,1152]{1,0:T(4,128)(4,1)S(1)} %bitcast.178, bf16[16,128,8,64]{1,3,2,0:T(8,128)(2,1)S(1)} %copy-done.6, s32[]{:T(128)S(6)} %select_n.523), kind=kOutput, calls=%fused_computation.165.clone.1 | convolution fusion | flops 618131456 | bytes 24138244 | tf_op jit(solution)/shard_map/while/body/eval_jaxpr/bqhd,bkhd->bhqk/dot_general | solution.py:153
  830.1 11.6 %copy.223 = bf16[4,5,128,1024]{2,1,3,0:T(8,128)(2,1)} copy(bf16[4,5,128,1024]{3,2,1,0:T(8,128)(2,1)} %bitcast.168) | data formatting | bytes 10485760 | tf_op jit(solution)/shard_map/while/body/eval_jaxpr/jit(_take)/gather | solution.py:141
  849.7 11.9 %pad_maximum_fusion.6 = (bf16[4,9,128,512]{2,1,3,0:T(8,128)(2,1)}, bf16[4,9,128,512]{2,1,3,0:T(8,128)(2,1)}) fusion(bf16[4,4,128,1024]{2,1,3,0:T(4,128)(2,1)S(1)} %bitcast.169, bf16[4,5,128,1024]{2,1,3,0:T(8,128)(2,1)} %broadcast_select_fusion.2), kind=kLoop, calls=%fused_computation.19.clone.1 | loop fusion | flops 18874368 | bytes 18874368 | tf_op jit(solution)/shard_map/while/body/eval_jaxpr/concatenate | solution.py:147
  872.3 10.9 %reshape.845 = bf16[4,1152,8,64]{1,3,2,0:T(8,128)(2,1)} reshape(bf16[4,9,128,512]{2,1,3,0:T(8,128)(2,1)} %get-tuple-element.500) | data formatting | bytes 9437184 | tf_op jit(solution)/shard_map/while/body/eval_jaxpr/reshape | solution.py:148
  883.2 11.5 %fusion.98 = (f32[4,8,128]{2,1,0:T(8,128)S(1)}, f32[4,8,128,1152]{3,2,1,0:T(8,128)}) fusion(bf16[4,1152,8,64]{1,3,2,0:T(8,128)(2,1)} %reshape.845, pred[4,1152]{1,0:T(4,128)(4,1)S(1)} %bitcast.178, bf16[16,128,8,64]{1,3,2,0:T(8,128)(2,1)S(1)} %copy-done.6, s32[]{:T(128)S(6)} %select_n.523), kind=kOutput, calls=%fused_computation.165.clone.1 | convolution fusion | flops 618131456 | bytes 24138244 | tf_op jit(solution)/shard_map/while/body/eval_jaxpr/bqhd,bkhd->bhqk/dot_general | solution.py:153
  (236 shorter events, 338.4 us)
Async XLA Ops:
  0.6 55.4 %copy-start = (bf16[512,512]{1,0:T(8,128)(2,1)S(1)}, bf16[512,512]{1,0:T(8,128)(2,1)}, u32[]{:S(2)}) copy-start(bf16[512,512]{1,0:T(8,128)(2,1)} %param.16) | copy-start | bytes 1572868
  26.2 12.0 %copy-start.10 = (bf16[512,512]{1,0:T(8,128)(2,1)S(1)}, bf16[512,512]{1,0:T(8,128)(2,1)}, u32[]{:S(2)}) copy-start(bf16[512,512]{1,0:T(8,128)(2,1)} %param.17) | copy-start | bytes 1572868
  26.2 13.1 %copy-start.3 = (bf16[4,4,128,512]{3,2,1,0:T(8,128)(2,1)S(1)}, bf16[4,4,128,512]{3,2,1,0:T(8,128)(2,1)}, u32[]{:S(2)}) copy-start(bf16[4,4,128,512]{3,2,1,0:T(8,128)(2,1)} %param.14) | copy-start | bytes 6291460
  26.2 431.4 %all-to-all-start = ((bf16[128,1,128,512]{3,2,1,0:T(8,128)(2,1)}), bf16[128,1,128,512]{3,2,1,0:T(8,128)(2,1)}, u32[]{:S(2)}, u32[]{:S(2)}) async-start(bf16[128,1,128,512]{3,2,1,0:T(8,128)(2,1)} %fusion.29), calls=%async_computation | async-start | bytes 33554432 | tf_op jit(solution)/shard_map/all_to_all | solution.py:98
  43.8 12.3 %copy-start.14 = (bf16[4,512]{1,0:T(4,128)(2,1)S(1)}, bf16[4,512]{1,0:T(4,128)(2,1)}, u32[]{:S(2)}) copy-start(bf16[4,512]{1,0:T(4,128)(2,1)} %param.15) | copy-start | bytes 12292
  43.8 12.5 %copy-start.13 = (s32[4,4,128]{2,1,0:T(4,128)S(1)}, s32[4,4,128]{2,1,0:T(4,128)}, u32[]{:S(2)}) copy-start(s32[4,4,128]{2,1,0:T(4,128)} %param.22) | copy-start | bytes 24580
  47.5 316.4 %collective-permute-start.1 = (bf16[1,4,128,1024]{3,2,1,0:T(8,128)(2,1)}, bf16[1,4,128,1024]{3,2,1,0:T(8,128)(2,1)}, u32[]{:S(2)}, u32[]{:S(2)}) collective-permute-start(bf16[1,4,128,1024]{3,2,1,0:T(8,128)(2,1)} %bitcast.181), channel_id=1, source_target_pairs={{8,0},{16,8},{24,16},{32,24},{40,32},{48,40},{56,48},{64,56},{72,6... | collective-permute-start | bytes 3145736 | tf_op jit(solution)/shard_map/ppermute | solution.py:28
  51.1 312.8 %collective-permute-start = (bf16[1,4,128,1024]{3,2,1,0:T(8,128)(2,1)}, bf16[1,4,128,1024]{3,2,1,0:T(8,128)(2,1)}, u32[]{:S(2)}, u32[]{:S(2)}) collective-permute-start(bf16[1,4,128,1024]{3,2,1,0:T(8,128)(2,1)} %bitcast.182), channel_id=1, source_target_pairs={{0,8},{8,16},{16,24},{24,32},{32,40},{40,48},{48,56},{56,64},{64,7... | collective-permute-start | bytes 3145736 | tf_op jit(solution)/shard_map/ppermute | solution.py:25
  56.3 283.6 %copy-start.16 = (s32[4,4,4]{2,1,0:T(4,128)S(1)}, s32[4,4,4]{2,1,0:T(4,128)}, u32[]{:S(2)}) copy-start(s32[4,4,4]{2,1,0:T(4,128)} %param.20) | copy-start | bytes 772
  363.8 10.7 %copy-start.9 = (bf16[2048,512]{1,0:T(8,128)(2,1)S(1)}, bf16[2048,512]{1,0:T(8,128)(2,1)}, u32[]{:S(2)}) copy-start(bf16[2048,512]{1,0:T(8,128)(2,1)} %convolution_convert_fusion.1) | copy-start | bytes 6291460
  367.8 81.8 %collective-permute-start.2 = (bf16[6,1,128,1024]{3,2,1,0:T(8,128)(2,1)}, bf16[6,1,128,1024]{3,2,1,0:T(8,128)(2,1)}, u32[]{:S(2)}, u32[]{:S(2)}) collective-permute-start(bf16[6,1,128,1024]{3,2,1,0:T(8,128)(2,1)} %get-tuple-element.389), channel_id=1, source_target_pairs={{0,1},{1,2},{2,3},{3,4},{4,5},{5,6},{6,7},{8,9},{9,10},{10,11},{11... | collective-permute-start | bytes 4718600 | tf_op jit(solution)/shard_map/ppermute | solution.py:25
  371.8 77.9 %collective-permute-start.3 = (bf16[6,1,128,1024]{3,2,1,0:T(8,128)(2,1)}, bf16[6,1,128,1024]{3,2,1,0:T(8,128)(2,1)}, u32[]{:S(2)}, u32[]{:S(2)}) collective-permute-start(bf16[6,1,128,1024]{3,2,1,0:T(8,128)(2,1)} %get-tuple-element.390), channel_id=1, source_target_pairs={{1,0},{2,1},{3,2},{4,3},{5,4},{6,5},{7,6},{9,8},{10,9},{11,10},{12... | collective-permute-start | bytes 4718600 | tf_op jit(solution)/shard_map/ppermute | solution.py:28
  374.5 74.4 %copy-start.11 = (bf16[512,512]{1,0:T(8,128)(2,1)S(1)}, bf16[512,512]{1,0:T(8,128)(2,1)}, u32[]{:S(2)}) copy-start(bf16[512,512]{1,0:T(8,128)(2,1)} %param.19) | copy-start | bytes 1572868
  473.6 11.7 %copy-start.15 = (s32[5]{0:T(128)S(1)}, s32[5]{0:T(128)}, u32[]{:S(2)}) copy-start(s32[5]{0:T(128)} %constant.326.clone..sunk.3) | copy-start | bytes 64
  485.3 433.6 %copy-start.12 = (bf16[512,512]{1,0:T(8,128)(2,1)S(1)}, bf16[512,512]{1,0:T(8,128)(2,1)}, u32[]{:S(2)}) copy-start(bf16[512,512]{1,0:T(8,128)(2,1)} %param.19) | copy-start | bytes 1572868
  485.3 14.4 %copy-start.5 = (bf16[16,128,8,64]{1,3,2,0:T(8,128)(2,1)}, bf16[16,128,8,64]{1,3,2,0:T(8,128)(2,1)S(1)}, u32[]{:S(2)}) copy-start(bf16[16,128,8,64]{1,3,2,0:T(8,128)(2,1)S(1)} %get-tuple-element.541) | copy-start | bytes 6291460 | tf_op jit(solution)/shard_map/while
  519.0 8.0 copy-start.2
  549.6 10.9 %copy-start.6 = (bf16[16,128,8,64]{1,3,2,0:T(8,128)(2,1)S(1)}, bf16[16,128,8,64]{1,3,2,0:T(8,128)(2,1)}, u32[]{:S(2)}) copy-start(bf16[16,128,8,64]{1,3,2,0:T(8,128)(2,1)} %copy-done.5) | copy-start | bytes 6291460 | tf_op jit(solution)/shard_map/while
  592.8 14.4 %copy-start.5 = (bf16[16,128,8,64]{1,3,2,0:T(8,128)(2,1)}, bf16[16,128,8,64]{1,3,2,0:T(8,128)(2,1)S(1)}, u32[]{:S(2)}) copy-start(bf16[16,128,8,64]{1,3,2,0:T(8,128)(2,1)S(1)} %get-tuple-element.541) | copy-start | bytes 6291460 | tf_op jit(solution)/shard_map/while
  657.2 10.9 %copy-start.6 = (bf16[16,128,8,64]{1,3,2,0:T(8,128)(2,1)S(1)}, bf16[16,128,8,64]{1,3,2,0:T(8,128)(2,1)}, u32[]{:S(2)}) copy-start(bf16[16,128,8,64]{1,3,2,0:T(8,128)(2,1)} %copy-done.5) | copy-start | bytes 6291460 | tf_op jit(solution)/shard_map/while
  700.4 14.4 %copy-start.5 = (bf16[16,128,8,64]{1,3,2,0:T(8,128)(2,1)}, bf16[16,128,8,64]{1,3,2,0:T(8,128)(2,1)S(1)}, u32[]{:S(2)}) copy-start(bf16[16,128,8,64]{1,3,2,0:T(8,128)(2,1)S(1)} %get-tuple-element.541) | copy-start | bytes 6291460 | tf_op jit(solution)/shard_map/while
  764.7 10.9 %copy-start.6 = (bf16[16,128,8,64]{1,3,2,0:T(8,128)(2,1)S(1)}, bf16[16,128,8,64]{1,3,2,0:T(8,128)(2,1)}, u32[]{:S(2)}) copy-start(bf16[16,128,8,64]{1,3,2,0:T(8,128)(2,1)} %copy-done.5) | copy-start | bytes 6291460 | tf_op jit(solution)/shard_map/while
  807.9 14.4 %copy-start.5 = (bf16[16,128,8,64]{1,3,2,0:T(8,128)(2,1)}, bf16[16,128,8,64]{1,3,2,0:T(8,128)(2,1)S(1)}, u32[]{:S(2)}) copy-start(bf16[16,128,8,64]{1,3,2,0:T(8,128)(2,1)S(1)} %get-tuple-element.541) | copy-start | bytes 6291460 | tf_op jit(solution)/shard_map/while
  872.3 10.9 %copy-start.6 = (bf16[16,128,8,64]{1,3,2,0:T(8,128)(2,1)S(1)}, bf16[16,128,8,64]{1,3,2,0:T(8,128)(2,1)}, u32[]{:S(2)}) copy-start(bf16[16,128,8,64]{1,3,2,0:T(8,128)(2,1)} %copy-done.5) | copy-start | bytes 6291460 | tf_op jit(solution)/shard_map/while
  (7 other events, 40.7 us)
where the time goes:
time: 929 us; the launch traced here: 923 us
  blocking collectives  343 us (37%)
  local copies, waits for them, and re-layouts  284 us (31%)
  other arithmetic  150 us (16%)
  matrix products  118 us (13%)
  starting transfers between devices  24.2 us (3%)
    pmax x1, blocking collectives, shards(): top = jnp.maximum(lax.pmax(local_top, ('row', 'col')), own_score)  277 us
    gather x8, local copies, waits for them, and re-layouts, attend(): jnp.take(padded_flat, (centre[:, None] + offsets[None, :]).reshape(-1), a...  77.4 us
    psum x1, blocking collectives, shards(): total, accum = lax.psum((local_total, local_accum), ('row', 'col'))  66.1 us
    dynamic_slice x8, local copies, waits for them, and re-layouts, attend(): lax.dynamic_slice_in_dim(remote, first, GROUP_BLOCKS, 1)  49.1 us
    concatenate x4, other arithmetic, attend(): gathered = jnp.concatenate([nearby, distant], axis=1)  47.4 us
    dot_general x4, matrix products, attend(): jnp.einsum('bqhd,bkhd->bhqk', group_query, group_keys, preferred_element_...  46 us
    reshape x4, local copies, waits for them, and re-layouts, attend(): group_keys = gathered[..., :D].reshape(GROUP_BLOCKS, key_count, H, HD)  43.7 us
    reshape x4, local copies, waits for them, and re-layouts, attend(): group_values = gathered[..., D:].reshape(GROUP_BLOCKS, key_count, H, HD)  43.1 us
  transfers between devices with their start and end apart: 5, of which 0 were waited for; matrix products, arithmetic and copies ran while one was open for 7% of the time, Pallas kernels for 0%

commit v1 on v0

v1 whole, which is shorter than its diff:
```python
import functools
import math

import jax
import jax.numpy as jnp
from jax import lax
from jax.experimental import pallas as pl
from jax.experimental.pallas import tpu as pltpu
from jax.sharding import PartitionSpec as P


D = 512
H = 8
HD = 64
BLK = 128
NEXP = 4
NVIRT = 4
PAIRS = H // 2
NEG_FILL = -1e30
SPLIT = (96, 32)
AXES = ("row", "col")
F32 = jnp.float32
BF16 = jnp.bfloat16


def dot_nt(a, b):
    return lax.dot_general(a, b, (((1,), (1,)), ((), ())), preferred_element_type=F32)


def dot_nn(a, b):
    return jnp.dot(a, b, preferred_element_type=F32)


def device_of(partner, blocks_x, blocks_y, mesh_cols):
    grid_cols = blocks_y * mesh_cols
    return partner // grid_cols // blocks_x * mesh_cols + partner % grid_cols // blocks_y


def send_kernel(blocks_y, where_to, partners, feats, *refs):
    nblocks = feats.shape[0]
    outs, (held, in_sem, out_sems) = refs[: len(SPLIT)], refs[len(SPLIT) :]
    pltpu.make_async_copy(feats, held, in_sem).start()
    pltpu.make_async_copy(feats, held, in_sem).wait()
    first = 0
    for part, rows in enumerate(SPLIT):
        for m in range(NEXP):
            for block in range(nblocks):
                dest = where_to(partners[block // blocks_y, block % blocks_y, m])
                pltpu.make_async_copy(
                    held.at[block, pl.ds(first, rows)], outs[part].at[dest], out_sems.at[part]
                ).start()
        first += rows
    for part in range(len(SPLIT)):
        every = outs[part].at[pl.ds(0, nblocks * NEXP)]
        pltpu.make_async_copy(every, every, out_sems.at[part]).wait()


def pair_query(query_t, pair):
    both = query_t[pair * 2 * HD : (pair + 1) * 2 * HD, :]
    upper = lax.broadcasted_iota(jnp.int32, both.shape, 0) < HD
    zero = jnp.zeros_like(both)
    return jnp.concatenate([jnp.where(upper, both, zero), jnp.where(upper, zero, both)], axis=1)


def diagonal(mixed):
    return mixed[:HD, :BLK], mixed[HD:, BLK:]


def project_keys(rows, w_key, w_value_t, keys, values_t):
    gathered = rows[...]
    keys[...] = dot_nn(gathered, w_key[...]).astype(BF16)
    values_t[...] = dot_nt(w_value_t[...], gathered).astype(BF16)


def local_kernel(
    live, own, up, down, left, right, ids, w_query_t, w_key, w_value_t, virt_key, virt_value_t,
    virt_query, query_out, acc_out, top_out, total_out, virt_out, rows, keys, values_t,
    virt_top, virt_total, virt_acc,
):
    step = pl.program_id(0)
    sources = (own, up, down, left, right)
    for slot, source in enumerate(sources):
        rows[slot * BLK : (slot + 1) * BLK, :] = source[0]
    project_keys(rows, w_key, w_value_t, keys, values_t)
    query_t = (dot_nt(w_query_t[...], own[0]) * (1.0 / math.sqrt(HD))).astype(BF16)
    query_out[0] = query_t
    chosen = ids[0]
    chosen_pair = jnp.concatenate([chosen, chosen], axis=1)
    for pair in range(PAIRS):
        lanes = slice(pair * 2 * HD, (pair + 1) * 2 * HD)
        query = pair_query(query_t, pair)
        scores = dot_nn(keys[:, lanes], query)
        pieces = [scores[:BLK]]
        for slot in range(1, 5):
            alive = live[step // 4, step % 4, slot - 1] == 1
            pieces.append(jnp.where(alive, scores[slot * BLK : (slot + 1) * BLK], NEG_FILL))
        virt_scores = dot_nn(virt_key[:, lanes], query)
        member = lax.broadcasted_iota(jnp.int32, virt_scores.shape, 0) == chosen_pair
        virt_scores = jnp.where(member, virt_scores, NEG_FILL)
        top = jnp.max(virt_scores, axis=0, keepdims=True)
        for piece in pieces:
            top = jnp.maximum(top, jnp.max(piece, axis=0, keepdims=True))
        virt_shares = jnp.exp(virt_scores - top)
        total = jnp.sum(virt_shares, axis=0, keepdims=True)
        mixed = dot_nn(virt_value_t[lanes, :], virt_shares.astype(BF16))
        shares = [jnp.exp(piece - top) for piece in pieces]
        for share in shares:
            total = total + jnp.sum(share, axis=0, keepdims=True)
        weights = jnp.concatenate([share.astype(BF16) for share in shares], axis=0)
        mixed = mixed + dot_nn(values_t[lanes, :], weights)
        for half, part in enumerate(diagonal(mixed)):
            head = 2 * pair + half
            acc_out[0, head * HD : (head + 1) * HD, :] = part
            top_out[0, head : head + 1, :] = top[:, half * BLK : (half + 1) * BLK]
            total_out[0, head : head + 1, :] = total[:, half * BLK : (half + 1) * BLK]

    @pl.when(step == 0)
    def _():
        virt_top[...] = jnp.full_like(virt_top, NEG_FILL)
        virt_total[...] = jnp.zeros_like(virt_total)
        virt_acc[...] = jnp.zeros_like(virt_acc)

    scores = dot_nt(virt_query[...], keys[:BLK, :])
    member = lax.broadcasted_iota(jnp.int32, scores.shape, 0) // H == chosen
    scores = jnp.where(member, scores, NEG_FILL)
    before = virt_top[:, :1]
    top = jnp.maximum(before, jnp.max(scores, axis=1, keepdims=True))
    fade = jnp.exp(before - top)
    shares = jnp.where(member, jnp.exp(scores - top), 0.0)
    virt_top[...] = jnp.broadcast_to(top, virt_top.shape)
    virt_total[...] = virt_total[...] * fade + jnp.sum(shares, axis=1, keepdims=True)
    values = values_t[:, :BLK]
    gained = virt_acc[...] * fade
    for _ in range(3):
        rounded = shares.astype(BF16)
        gained = gained + dot_nt(rounded, values)
        shares = shares - rounded.astype(F32)
    virt_acc[...] = gained

    @pl.when(step == pl.num_programs(0) - 1)
    def _():
        head_of_lane = lax.broadcasted_iota(jnp.int32, (H, D), 1) // HD
        own_head = head_of_lane == lax.broadcasted_iota(jnp.int32, (H, D), 0)
        for v in range(NVIRT):
            heads = slice(v * H, (v + 1) * H)
            for kind, held in enumerate(
                (
                    jnp.broadcast_to(virt_top[heads, :1], (H, D)),
                    jnp.broadcast_to(virt_total[heads, :1], (H, D)),
                    virt_acc[heads, :],
                )
            ):
                row = kind * NVIRT + v
                virt_out[row : row + 1, :] = jnp.sum(
                    jnp.where(own_head, held, 0.0), axis=0, keepdims=True
                )


def remote_kernel(last, partners, *refs):
    sources, refs = refs[:NEXP], refs[NEXP:]
    query_in, acc_in, top_in, total_in, w_key, w_value_t = refs[:6]
    refs = refs[6:]
    if last:
        feats, w_out, node_out, rows, keys, values_t, context = refs
    else:
        acc_out, top_out, total_out, rows, keys, values_t = refs
    count = sources[0].shape[1]
    for slot, source in enumerate(sources):
        rows[slot * count : (slot + 1) * count, :] = source[0]
    project_keys(rows, w_key, w_value_t, keys, values_t)
    query_t = query_in[0]
    for pair in range(PAIRS):
        lanes = slice(pair * 2 * HD, (pair + 1) * 2 * HD)
        query = pair_query(query_t, pair)
        scores = dot_nn(keys[:, lanes], query)
        pick = slice(2 * pair, 2 * pair + 1)
        pick_next = slice(2 * pair + 1, 2 * pair + 2)
        before = jnp.concatenate([top_in[0, pick, :], top_in[0, pick_next, :]], axis=1)
        total = jnp.concatenate([total_in[0, pick, :], total_in[0, pick_next, :]], axis=1)
        top = jnp.maximum(before, jnp.max(scores, axis=0, keepdims=True))
        fade = jnp.exp(before - top)
        shares = jnp.exp(scores - top)
        total = total * fade + jnp.sum(shares, axis=0, keepdims=True)
        mixed = dot_nn(values_t[lanes, :], shares.astype(BF16))
        for half, part in enumerate(diagonal(mixed)):
            head = 2 * pair + half
            nodes = slice(half * BLK, (half + 1) * BLK)
            features = slice(head * HD, (head + 1) * HD)
            gained = acc_in[0, features, :] * fade[:, nodes] + part
            if last:
                context[features, :] = (gained / total[:, nodes]).astype(BF16)
            else:
                acc_out[0, features, :] = gained
                top_out[0, head : head + 1, :] = top[:, nodes]
                total_out[0, head : head + 1, :] = total[:, nodes]
    if last:
        mixed = lax.dot_general(
            context[...], w_out[...], (((0,), (0,)), ((), ())), preferred_element_type=F32
        )
        node_out[0] = (feats[0].astype(F32) + mixed).astype(BF16)


def turn(index, stride, size, shift):
    place = index // stride % size
    return index + ((place + shift) % size - place) * stride


def in_order(parts, place):
    size = len(parts)
    ordered = []
    for source in range(size):
        chosen = parts[0]
        for shift in range(1, size):
            chosen = jnp.where((place - source) % size == shift, parts[shift], chosen)
        ordered.append(chosen)
    return ordered


def merge(parts):
    tops = [part[:NVIRT] for part in parts]
    top = functools.reduce(jnp.maximum, tops)
    fades = [jnp.exp(one - top) for one in tops]
    sums = [
        sum(part[kind * NVIRT : (kind + 1) * NVIRT] * fade for part, fade in zip(parts, fades))
        for kind in (1, 2)
    ]
    return jnp.concatenate([top, *sums], axis=0)


def halo(feats):
    count_x, count_y = lax.axis_size("row"), lax.axis_size("col")

    def shift(edge, axis, count, step):
        pairs = [(i, i + step) for i in range(count) if 0 <= i + step < count]
        return lax.ppermute(edge, axis, pairs)

    return (
        shift(feats[-1], "row", count_x, 1),
        shift(feats[0], "row", count_x, -1),
        shift(feats[:, -1], "col", count_y, 1),
        shift(feats[:, 0], "col", count_y, -1),
    )


def shards(feats, virt_emb, w_query, w_key, w_value, w_out, link_mask, partners, virt_ids):
    blocks_x, blocks_y = feats.shape[0], feats.shape[1]
    nblocks = blocks_x * blocks_y
    mesh_rows, mesh_cols = lax.axis_size("row"), lax.axis_size("col")
    devices = mesh_rows * mesh_cols
    where_to = functools.partial(
        device_of, blocks_x=blocks_x, blocks_y=blocks_y, mesh_cols=mesh_cols
    )
    flat = feats.reshape(nblocks, BLK, D)
    shapes = jax.ShapeDtypeStruct
    anywhere = pl.BlockSpec(memory_space=pl.ANY)

    edges = halo(feats)
    outgoing = pl.pallas_call(
        functools.partial(send_kernel, blocks_y, where_to),
        name="send",
        out_shape=[shapes((devices, rows, D), BF16) for rows in SPLIT],
        in_specs=[pl.BlockSpec(memory_space=pltpu.SMEM), anywhere],
        out_specs=[anywhere] * len(SPLIT),
        scratch_shapes=[
            pltpu.VMEM((nblocks, BLK, D), BF16),
            pltpu.SemaphoreType.DMA,
            pltpu.SemaphoreType.DMA((len(SPLIT),)),
        ],
        cost_estimate=pl.CostEstimate(flops=0, bytes_accessed=10 << 20, transcendentals=0),
    )(partners, flat)
    arrived = []
    for part, slots in enumerate(outgoing):
        arrived.append(lax.all_to_all(slots, AXES, split_axis=0, concat_axis=0, tiled=True))

    w_query_t, w_value_t = w_query.T, w_value.T
    scale = 1.0 / math.sqrt(HD)
    virt_rows = jnp.dot(
        virt_emb, jnp.concatenate([w_query, w_key, w_value], axis=1), preferred_element_type=F32
    ).astype(BF16)
    virt_query, virt_key, virt_value = virt_rows[:, :D], virt_rows[:, D : 2 * D], virt_rows[:, 2 * D :]
    pad_to = 8
    virt_key_rows = jnp.pad(virt_key, ((0, pad_to - NVIRT), (0, 0)))
    virt_value_cols = jnp.pad(virt_value, ((0, pad_to - NVIRT), (0, 0))).T
    head_of_lane = jnp.arange(D) // HD
    own_head = head_of_lane[None, :] == jnp.arange(H)[:, None]
    virt_query_rows = jnp.where(
        own_head[None], virt_query[:, None, :] * jnp.asarray(scale, BF16), jnp.zeros((), BF16)
    ).reshape(NVIRT * H, D)

    row_ids = lax.axis_index("row") * blocks_x + jnp.arange(blocks_x, dtype=jnp.int32)[:, None]
    col_ids = lax.axis_index("col") * blocks_y + jnp.arange(blocks_y, dtype=jnp.int32)[None, :]
    inside = jnp.stack(
        [
            jnp.broadcast_to(row_ids > 0, (blocks_x, blocks_y)),
            jnp.broadcast_to(row_ids < mesh_rows * blocks_x - 1, (blocks_x, blocks_y)),
            jnp.broadcast_to(col_ids > 0, (blocks_x, blocks_y)),
            jnp.broadcast_to(col_ids < mesh_cols * blocks_y - 1, (blocks_x, blocks_y)),
        ],
        axis=-1,
    )
    live = ((link_mask == 1) & inside).astype(jnp.int32)

    padded = jnp.concatenate([flat, *edges], axis=0)
    start_up = nblocks
    start_down = start_up + blocks_y
    start_left = start_down + blocks_y
    start_right = start_left + blocks_x

    def above(b, *_):
        return (jnp.where(b < blocks_y, start_up + b, b - blocks_y), 0, 0)

    def below(b, *_):
        near = b - (nblocks - blocks_y)
        return (jnp.where(near >= 0, start_down + near, b + blocks_y), 0, 0)

    def before(b, *_):
        return (jnp.where(b % blocks_y == 0, start_left + b // blocks_y, b - 1), 0, 0)

    def after(b, *_):
        return (jnp.where(b % blocks_y == blocks_y - 1, start_right + b // blocks_y, b + 1), 0, 0)

    def same(b, *_):
        return (b, 0, 0)

    def whole(shape):
        return pl.BlockSpec(shape, lambda b, *_: (0,) * len(shape))

    block = (1, BLK, D)
    turned = (1, D, BLK)
    stats = (1, H, BLK)
    weight = whole((D, D))
    state_shapes = [
        shapes((nblocks, D, BLK), F32), shapes((nblocks, H, BLK), F32), shapes((nblocks, H, BLK), F32)
    ]
    state_specs = [pl.BlockSpec(turned, same), pl.BlockSpec(stats, same), pl.BlockSpec(stats, same)]
    local_keys = 5 * BLK
    query_t, *state, virt_part = pl.pallas_call(
        local_kernel,
        name="local",
        out_shape=[shapes((nblocks, D, BLK), BF16), *state_shapes, shapes((3 * NVIRT, D), F32)],
        grid_spec=pltpu.PrefetchScalarGridSpec(
            num_scalar_prefetch=1,
            grid=(nblocks,),
            in_specs=[
                *(pl.BlockSpec(block, index) for index in (same, above, below, before, after)),
                pl.BlockSpec((1, 1, BLK), same),
                weight, weight, weight,
                whole((pad_to, D)), whole((D, pad_to)), whole((NVIRT * H, D)),
            ],
            out_specs=[pl.BlockSpec(turned, same), *state_specs, whole((3 * NVIRT, D))],
            scratch_shapes=[
                pltpu.VMEM((local_keys, D), BF16),
                pltpu.VMEM((local_keys, D), BF16),
                pltpu.VMEM((D, local_keys), BF16),
                pltpu.VMEM((NVIRT * H, BLK), F32),
                pltpu.VMEM((NVIRT * H, BLK), F32),
                pltpu.VMEM((NVIRT * H, D), F32),
            ],
        ),
        cost_estimate=pl.CostEstimate(
            flops=40_000_000_000, bytes_accessed=30 << 20, transcendentals=nblocks * H * BLK * local_keys
        ),
    )(
        live, padded, padded, padded, padded, padded, virt_ids.reshape(nblocks, 1, BLK),
        w_query_t, w_key, w_value_t, virt_key_rows, virt_value_cols, virt_query_rows,
    )

    def partner_block(m):
        def index(b, partner):
            return (where_to(partner[b // blocks_y, b % blocks_y, m]), 0, 0)

        return index

    node_out = None
    for part, rows in enumerate(SPLIT):
        last = part == len(SPLIT) - 1
        in_specs = [
            *(pl.BlockSpec((1, rows, D), partner_block(m)) for m in range(NEXP)),
            pl.BlockSpec(turned, same), *state_specs, weight, weight,
        ]
        operands = [*[arrived[part]] * NEXP, query_t, *state, w_key, w_value_t]
        scratch = [
            pltpu.VMEM((NEXP * rows, D), BF16),
            pltpu.VMEM((NEXP * rows, D), BF16),
            pltpu.VMEM((D, NEXP * rows), BF16),
        ]
        if last:
            in_specs += [pl.BlockSpec(block, same), weight]
            operands += [flat, w_out]
            out_shape, out_specs = shapes(flat.shape, BF16), pl.BlockSpec(block, same)
            scratch += [pltpu.VMEM((D, BLK), BF16)]
        else:
            out_shape, out_specs = state_shapes, state_specs
        result = pl.pallas_call(
            functools.partial(remote_kernel, last),
            out_shape=out_shape,
            grid_spec=pltpu.PrefetchScalarGridSpec(
                num_scalar_prefetch=1, grid=(nblocks,), in_specs=in_specs, out_specs=out_specs,
                scratch_shapes=scratch,
            ),
            cost_estimate=pl.CostEstimate(
                flops=25_000_000_000 * rows // BLK,
                bytes_accessed=20 << 20,
                transcendentals=nblocks * H * BLK * NEXP * rows,
            ),
        )(partners, *operands)
        if last:
            node_out = result
        else:
            state = result

    own_score = (
        jnp.sum((virt_query.astype(F32) * virt_key.astype(F32)).reshape(NVIRT, H, HD), axis=-1) * scale
    )
    own_score = jnp.repeat(own_score, HD, axis=1)
    part = virt_part
    ways = (("col", mesh_cols, 1, 2), ("col", mesh_cols, 2, 4), ("row", mesh_rows, 4, 4), ("row", mesh_rows, 1, 4))
    for axis, count, stride, size in ways:
        others = [
            lax.ppermute(part, axis, [(i, turn(i, stride, size, shift)) for i in range(count)])
            for shift in range(1, size)
        ]
        part = merge(in_order([part, *others], lax.axis_index(axis) // stride % size))
    own = jnp.concatenate([own_score, jnp.ones_like(own_score), virt_value.astype(F32)], axis=0)
    part = merge([part, own])
    virt_context = (part[2 * NVIRT :] / part[NVIRT : 2 * NVIRT]).astype(BF16)
    virt_out = virt_emb.astype(F32) + jnp.dot(virt_context, w_out, preferred_element_type=F32)
    return node_out.reshape(feats.shape), virt_out


def solution(mesh):
    return jax.shard_map(
        shards,
        mesh=mesh,
        in_specs=(
            P("row", "col", None, None),
            P(),
            P(),
            P(),
            P(),
            P(),
            P("row", "col", None),
            P("row", "col", None),
            P("row", "col", None),
        ),
        out_specs=(P("row", "col", None, None), P()),
        check_vma=False,
    )
```

time: 929 us -> 419 us (0.45)
  blocking collectives: 343 us -> 0 us
  local copies, waits for them, and re-layouts: 284 us -> 16.5 us
  waiting for transfers between devices: 0.02 us -> 198 us
  other arithmetic: 150 us -> 3.87 us
  Pallas kernels: 0 us -> 139 us
  matrix products: 118 us -> 2.18 us
  starting transfers between devices: 24.2 us -> 54.7 us
    pmax x1 -> x0, blocking collectives: 277 us -> none  [shards(): top = jnp.maximum(lax.pmax(local_top, ('row', 'col')), own_score)]
    ppermute x4 -> x14, waiting for transfers between devices: 0.02 us -> 198 us  [the longest x4 145 us: shift(): return lax.ppermute(edge, axis, pairs)]
    pallas_call x0 -> x4, Pallas kernels: none -> 139 us  [the longest x2 72.8 us: shards(): pl.pallas_call(functools.partial(remote_kernel, last), out_shape=out_shap...]
    dot_general x28 -> x2, matrix products: 118 us -> 2.18 us  [the longest x1 1.35 us: shards(): jnp.dot(virt_emb, jnp.concatenate([w_query, w_key, w_value], axis=1), pre...]
    reshape x19 -> x0, local copies, waits for them, and re-layouts: 105 us -> none  [the longest x4 43.7 us: attend(): group_keys = gathered[..., :D].reshape(GROUP_BLOCKS, key_count, H, HD)]
    gather x10 -> x0, local copies, waits for them, and re-layouts: 98.4 us -> none  [the longest x8 77.4 us: attend(): jnp.take(padded_flat, (centre[:, None] + offsets[None, :]).reshape(-1), a...]
    psum x1 -> x0, blocking collectives: 66.1 us -> none  [shards(): total, accum = lax.psum((local_total, local_accum), ('row', 'col'))]
    concatenate x5 -> x3, other arithmetic: 55.3 us -> 0.03 us  [merge(): return jnp.concatenate([top, *sums], axis=0)]
  transfers between devices with their start and end apart: 5 -> 16, of which waited for: 0 -> 9; matrix products, arithmetic and copies ran while one was open for 7% -> 5% of each run, Pallas kernels for 0% -> 25%
where the time goes in v1:
time: 419 us; the launch traced here: 416 us
  waiting for transfers between devices  198 us (47%)
  Pallas kernels  139 us (33%)
  starting transfers between devices  54.7 us (13%)
  local copies, waits for them, and re-layouts  16.5 us (4%)
    ppermute x4, waiting for transfers between devices, shift(): return lax.ppermute(edge, axis, pairs)  145 us
    pallas_call x2, Pallas kernels, shards(): pl.pallas_call(functools.partial(remote_kernel, last), out_shape=out_shap...  72.8 us
    pallas_call x1, Pallas kernels, shards(): pl.pallas_call(local_kernel, name='local', out_shape=[shapes((nblocks, D,...  60.9 us
    ppermute x10, waiting for transfers between devices, shards(): lax.ppermute(part, axis, [(i, turn(i, stride, size, shift)) for i in rang...  53.7 us
    all_to_all x2, starting transfers between devices, shards(): lax.all_to_all(slots, AXES, split_axis=0, concat_axis=0, tiled=True)  25 us
    ppermute x10, starting transfers between devices, shards(): lax.ppermute(part, axis, [(i, turn(i, stride, size, shift)) for i in rang...  17.6 us
    ppermute x4, starting transfers between devices, shift(): return lax.ppermute(edge, axis, pairs)  12.1 us
    unnamed x17, local copies, waits for them, and re-layouts  10.3 us
  transfers between devices with their start and end apart: 16, of which 9 were waited for; matrix products, arithmetic and copies ran while one was open for 5% of the time, Pallas kernels for 25%

profile of v1, /device:TPU:1, one launch (start us, length us, event | category | flops | bytes accessed | tf_op | source)
XLA Modules:
  0.0 415.8 jit_solution(822745847447787017)
XLA Ops:
  0.6 5.6 %send.1 = (bf16[128,96,512]{2,1,0:T(8,128)(2,1)}, bf16[128,32,512]{2,1,0:T(8,128)(2,1)}) custom-call(s32[4,4,4]{2,1,0:T(4,128)} %partners.5, bf16[16,128,512]{2,1,0:T(8,128)(2,1)} %bitcast.44), custom_call_target="tpu_custom_call" | custom-call | bytes 10485760 | tf_op jit(solution)/shard_map/send/pallas_call | solution.py:258
  6.3 11.9 %all-to-all-start.1 = ((bf16[128,96,512]{2,1,0:T(8,128)(2,1)}), bf16[128,96,512]{2,1,0:T(8,128)(2,1)}, u32[]{:S(2)}, u32[]{:S(2)}) async-start(bf16[128,96,512]{2,1,0:T(8,128)(2,1)} %get-tuple-element.14), calls=%async_computation.1 | async-start | bytes 25165824 | tf_op jit(solution)/shard_map/all_to_all | solution.py:273
  20.5 4.8 %collective-permute-start = (bf16[4,128,512]{2,1,0:T(8,128)(2,1)}, bf16[4,128,512]{2,1,0:T(8,128)(2,1)}, u32[]{:S(2)}, u32[]{:S(2)}) collective-permute-start(bf16[4,128,512]{2,1,0:T(8,128)(2,1)} %get-tuple-element.31), channel_id=1, source_target_pairs={{0,8},{8,16},{16,24},{24,32},{32,40},{40,48},{48,56},{56,64},{64,7... | collective-permute-start | bytes 1572872 | tf_op jit(solution)/shard_map/ppermute | solution.py:235
  26.5 3.6 collective-permute-start.3
  30.0 2.4 collective-permute-start.2
  35.9 2.0 copy.38
  42.5 100.9 %collective-permute-done = bf16[4,128,512]{2,1,0:T(8,128)(2,1)} collective-permute-done((bf16[4,128,512]{2,1,0:T(8,128)(2,1)}, bf16[4,128,512]{2,1,0:T(8,128)(2,1)}, u32[]{:S(2)}, u32[]{:S(2)}) %collective-permute-start) | collective-permute-done | bytes 524320 | tf_op jit(solution)/shard_map/ppermute | solution.py:235
  145.4 28.0 %collective-permute-done.1 = bf16[4,128,512]{2,1,0:T(8,128)(2,1)} collective-permute-done((bf16[4,128,512]{2,1,0:T(8,128)(2,1)}, bf16[4,128,512]{2,1,0:T(8,128)(2,1)}, u32[]{:S(2)}, u32[]{:S(2)}) %collective-permute-start.1) | collective-permute-done | bytes 524320 | tf_op jit(solution)/shard_map/ppermute | solution.py:235
  173.3 1.9 constant_dynamic-update-slice_fusion.2
  175.2 15.6 %collective-permute-done.2 = bf16[4,128,512]{2,1,0:T(8,128)(2,1)} collective-permute-done((bf16[4,128,512]{2,1,0:T(8,128)(2,1)}, bf16[4,128,512]{2,1,0:T(8,128)(2,1)}, u32[]{:S(2)}, u32[]{:S(2)}) %collective-permute-start.2) | collective-permute-done | bytes 524320 | tf_op jit(solution)/shard_map/ppermute | solution.py:235
  190.8 1.9 constant_dynamic-update-slice_fusion.1
  194.6 60.9 %local.1 = (bf16[16,512,128]{2,1,0:T(8,128)(2,1)}, f32[16,512,128]{2,1,0:T(8,128)}, f32[16,8,128]{2,1,0:T(8,128)}, f32[16,8,128]{2,1,0:T(8,128)}, f32[12,512]{1,0:T(8,128)}) custom-call(s32[4,4,4]{2,1,0:T(4,128)} %fusion.34.live, bf16[32,128,512]{2,1,0:T(8,128)(2,1)} %constant_dynamic-update-slice_fusion.own.up.down.left.right, ...), custom_call_target="tpu_custom_call" | custom-call | flops 40000000000 | bytes 31457280 | tf_op jit(solution)/shard_map/local/pallas_call | solution.py:337
  257.8 2.3 collective-permute-start.7
  260.1 2.5 collective-permute-start.5
  264.4 13.1 %all-to-all-start = ((bf16[128,32,512]{2,1,0:T(8,128)(2,1)}), bf16[128,32,512]{2,1,0:T(8,128)(2,1)}, u32[]{:S(2)}, u32[]{:S(2)}) async-start(bf16[128,32,512]{2,1,0:T(8,128)(2,1)} %get-tuple-element.12), calls=%async_computation | async-start | bytes 8388608 | tf_op jit(solution)/shard_map/all_to_all | solution.py:273
  279.0 2.5 collective-permute-start.9
  282.8 34.7 %collective-permute-done.10 = f32[12,512]{1,0:T(8,128)S(1)} collective-permute-done((f32[12,512]{1,0:T(8,128)S(1)}, f32[12,512]{1,0:T(8,128)S(1)}, u32[]{:S(2)}, u32[]{:S(2)}) %collective-permute-start.10) | collective-permute-done | bytes 24608 | tf_op jit(solution)/shard_map/ppermute | solution.py:420
  317.5 6.7 %collective-permute-done.9 = f32[12,512]{1,0:T(8,128)S(1)} collective-permute-done((f32[12,512]{1,0:T(8,128)S(1)}, f32[12,512]{1,0:T(8,128)S(1)}, u32[]{:S(2)}, u32[]{:S(2)}) %collective-permute-start.9) | collective-permute-done | bytes 24608 | tf_op jit(solution)/shard_map/ppermute | solution.py:420
  324.4 3.8 collective-permute-start.13
  328.3 2.1 collective-permute-start.12
  332.2 2.7 collective-permute-done.13
  334.9 6.5 %collective-permute-done.12 = f32[12,512]{0,1:T(8,128)S(1)} collective-permute-done((f32[12,512]{0,1:T(8,128)S(1)}, f32[12,512]{0,1:T(8,128)S(1)}, u32[]{:S(2)}, u32[]{:S(2)}) %collective-permute-start.12) | collective-permute-done | bytes 24608 | tf_op jit(solution)/shard_map/ppermute | solution.py:420
  343.0 41.8 %shard_map.104 = (f32[16,512,128]{2,1,0:T(8,128)}, f32[16,8,128]{2,1,0:T(8,128)}, f32[16,8,128]{2,1,0:T(8,128)}) custom-call(s32[4,4,4]{2,1,0:T(4,128)} %partners.5, bf16[128,96,512]{2,1,0:T(8,128)(2,1)} %all-to-all-done.1.refs_0_.refs_1_.refs_2_.refs_3_, bf16[128,96,512]{2,1,0:T(8,128)(2,1)} %all-to-all-done.1.refs_0_.refs_1_.refs_2_.refs_3_, ...), custom_call_target="tpu_custom_call" | custom-call | flops 18749999104 | bytes 20971520 | tf_op jit(solution)/shard_map/pallas_call | solution.py:394
  384.8 31.1 %shard_map.105 = bf16[16,128,512]{2,1,0:T(8,128)(2,1)} custom-call(s32[4,4,4]{2,1,0:T(4,128)} %partners.5, bf16[128,32,512]{2,1,0:T(8,128)(2,1)} %all-to-all-done.refs_0_.refs_1_.refs_2_.refs_3_, bf16[128,32,512]{2,1,0:T(8,128)(2,1)} %all-to-all-done.refs_0_.refs_1_.refs_2_.refs_3_, bf16[128,32,512]{2,1,0:T(8,128)(2,1)} %all-to-all-done.refs_0_.refs_1_.refs_2_.refs_3_, ...), custom_call_target="tpu_custom_call" | custom-call | flops 6249999872 | bytes 20971520 | tf_op jit(solution)/shard_map/pallas_call | solution.py:394
  (68 shorter events, 25.6 us)
Async XLA Ops:
  6.2 11.9 %copy-start = (bf16[4,4,128,512]{3,2,1,0:T(8,128)(2,1)S(1)}, bf16[4,4,128,512]{3,2,1,0:T(8,128)(2,1)}, u32[]{:S(2)}) copy-start(bf16[4,4,128,512]{3,2,1,0:T(8,128)(2,1)} %param.9) | copy-start | bytes 6291460
  6.3 258.1 %all-to-all-start.1 = ((bf16[128,96,512]{2,1,0:T(8,128)(2,1)}), bf16[128,96,512]{2,1,0:T(8,128)(2,1)}, u32[]{:S(2)}, u32[]{:S(2)}) async-start(bf16[128,96,512]{2,1,0:T(8,128)(2,1)} %get-tuple-element.14), calls=%async_computation.1 | async-start | bytes 25165824 | tf_op jit(solution)/shard_map/all_to_all | solution.py:273
  18.2 14.3 %copy-start.2 = (bf16[512,512]{1,0:T(8,128)(2,1)S(1)}, bf16[512,512]{1,0:T(8,128)(2,1)}, u32[]{:S(2)}) copy-start(bf16[512,512]{1,0:T(8,128)(2,1)} %refs_8_.3) | copy-start | bytes 1572868
  18.2 14.3 %copy-start.3 = (bf16[512,512]{1,0:T(8,128)(2,1)S(1)}, bf16[512,512]{1,0:T(8,128)(2,1)}, u32[]{:S(2)}) copy-start(bf16[512,512]{1,0:T(8,128)(2,1)} %param.11) | copy-start | bytes 1572868
  18.2 14.3 %copy-start.4 = (bf16[4,512]{1,0:T(4,128)(2,1)S(1)}, bf16[4,512]{1,0:T(4,128)(2,1)}, u32[]{:S(2)}) copy-start(bf16[4,512]{1,0:T(4,128)(2,1)} %param.10) | copy-start | bytes 12292
  19.3 154.1 %collective-permute-start.1 = (bf16[4,128,512]{2,1,0:T(8,128)(2,1)}, bf16[4,128,512]{2,1,0:T(8,128)(2,1)}, u32[]{:S(2)}, u32[]{:S(2)}) collective-permute-start(bf16[4,128,512]{2,1,0:T(8,128)(2,1)} %get-tuple-element.30), channel_id=1, source_target_pairs={{8,0},{16,8},{24,16},{32,24},{40,32},{48,40},{56,48},{64,56},{72,6... | collective-permute-start | bytes 1572872 | tf_op jit(solution)/shard_map/ppermute | solution.py:235
  20.5 122.9 %collective-permute-start = (bf16[4,128,512]{2,1,0:T(8,128)(2,1)}, bf16[4,128,512]{2,1,0:T(8,128)(2,1)}, u32[]{:S(2)}, u32[]{:S(2)}) collective-permute-start(bf16[4,128,512]{2,1,0:T(8,128)(2,1)} %get-tuple-element.31), channel_id=1, source_target_pairs={{0,8},{8,16},{16,24},{24,32},{32,40},{40,48},{48,56},{56,64},{64,7... | collective-permute-start | bytes 1572872 | tf_op jit(solution)/shard_map/ppermute | solution.py:235
  26.5 166.2 %collective-permute-start.3 = (bf16[4,128,512]{2,1,0:T(8,128)(2,1)}, bf16[4,128,512]{2,1,0:T(8,128)(2,1)}, u32[]{:S(2)}, u32[]{:S(2)}) collective-permute-start(bf16[4,128,512]{2,1,0:T(8,128)(2,1)} %get-tuple-element.28), channel_id=1, source_target_pairs={{1,0},{2,1},{3,2},{4,3},{5,4},{6,5},{7,6},{9,8},{10,9},{11,10},{12... | collective-permute-start | bytes 1572872 | tf_op jit(solution)/shard_map/ppermute | solution.py:235
  30.0 160.8 %collective-permute-start.2 = (bf16[4,128,512]{2,1,0:T(8,128)(2,1)}, bf16[4,128,512]{2,1,0:T(8,128)(2,1)}, u32[]{:S(2)}, u32[]{:S(2)}) collective-permute-start(bf16[4,128,512]{2,1,0:T(8,128)(2,1)} %get-tuple-element.29), channel_id=1, source_target_pairs={{0,1},{1,2},{2,3},{3,4},{4,5},{5,6},{6,7},{8,9},{9,10},{10,11},{11... | collective-permute-start | bytes 1572872 | tf_op jit(solution)/shard_map/ppermute | solution.py:235
  255.4 1.5 collective-permute-start.4
  257.8 4.8 %collective-permute-start.7 = (f32[12,512]{1,0:T(8,128)S(1)}, f32[12,512]{1,0:T(8,128)S(1)}, u32[]{:S(2)}, u32[]{:S(2)}) collective-permute-start(f32[12,512]{1,0:T(8,128)S(1)} %pad_maximum_fusion), channel_id=1, source_target_pairs={{0,2},{1,3},{2,4},{3,5},{4,6},{5,7},{6,0},{7,1},{8,10},{9,11},{10,... | collective-permute-start | bytes 73736 | tf_op jit(solution)/shard_map/ppermute | solution.py:420
  260.1 4.3 %collective-permute-start.6 = (f32[12,512]{1,0:T(8,128)S(1)}, f32[12,512]{1,0:T(8,128)S(1)}, u32[]{:S(2)}, u32[]{:S(2)}) collective-permute-start(f32[12,512]{1,0:T(8,128)S(1)} %pad_maximum_fusion), channel_id=1, source_target_pairs={{0,4},{1,5},{2,6},{3,7},{4,0},{5,1},{6,2},{7,3},{8,12},{9,13},{10,... | collective-permute-start | bytes 73736 | tf_op jit(solution)/shard_map/ppermute | solution.py:420
  260.1 4.3 %collective-permute-start.5 = (f32[12,512]{1,0:T(8,128)S(1)}, f32[12,512]{1,0:T(8,128)S(1)}, u32[]{:S(2)}, u32[]{:S(2)}) collective-permute-start(f32[12,512]{1,0:T(8,128)S(1)} %pad_maximum_fusion), channel_id=1, source_target_pairs={{0,6},{1,7},{2,0},{3,1},{4,2},{5,3},{6,4},{7,5},{8,14},{9,15},{10,... | collective-permute-start | bytes 73736 | tf_op jit(solution)/shard_map/ppermute | solution.py:420
  264.4 120.3 %all-to-all-start = ((bf16[128,32,512]{2,1,0:T(8,128)(2,1)}), bf16[128,32,512]{2,1,0:T(8,128)(2,1)}, u32[]{:S(2)}, u32[]{:S(2)}) async-start(bf16[128,32,512]{2,1,0:T(8,128)(2,1)} %get-tuple-element.12), calls=%async_computation | async-start | bytes 8388608 | tf_op jit(solution)/shard_map/all_to_all | solution.py:273
  277.5 64.6 %copy-start.1 = (bf16[512,512]{1,0:T(8,128)(2,1)S(1)}, bf16[512,512]{1,0:T(8,128)(2,1)}, u32[]{:S(2)}) copy-start(bf16[512,512]{1,0:T(8,128)(2,1)} %refs_11_.1) | copy-start | bytes 1572868
  277.6 39.9 %collective-permute-start.10 = (f32[12,512]{1,0:T(8,128)S(1)}, f32[12,512]{1,0:T(8,128)S(1)}, u32[]{:S(2)}, u32[]{:S(2)}) collective-permute-start(f32[12,512]{1,0:T(8,128)S(1)} %pad_maximum_fusion.1), channel_id=1, source_target_pairs={{0,32},{8,40},{16,48},{24,56},{32,64},{40,72},{48,80},{56,88},{64,... | collective-permute-start | bytes 73736 | tf_op jit(solution)/shard_map/ppermute | solution.py:420
  279.0 45.1 %collective-permute-start.9 = (f32[12,512]{1,0:T(8,128)S(1)}, f32[12,512]{1,0:T(8,128)S(1)}, u32[]{:S(2)}, u32[]{:S(2)}) collective-permute-start(f32[12,512]{1,0:T(8,128)S(1)} %pad_maximum_fusion.1), channel_id=1, source_target_pairs={{0,64},{8,72},{16,80},{24,88},{32,96},{40,104},{48,112},{56,120},{... | collective-permute-start | bytes 73736 | tf_op jit(solution)/shard_map/ppermute | solution.py:420
  281.5 42.7 %collective-permute-start.8 = (f32[12,512]{1,0:T(8,128)S(1)}, f32[12,512]{1,0:T(8,128)S(1)}, u32[]{:S(2)}, u32[]{:S(2)}) collective-permute-start(f32[12,512]{1,0:T(8,128)S(1)} %pad_maximum_fusion.1), channel_id=1, source_target_pairs={{0,96},{8,104},{16,112},{24,120},{32,0},{40,8},{48,16},{56,24},{64... | collective-permute-start | bytes 73736 | tf_op jit(solution)/shard_map/ppermute | solution.py:420
  324.4 10.4 %collective-permute-start.13 = (f32[12,512]{0,1:T(8,128)S(1)}, f32[12,512]{0,1:T(8,128)S(1)}, u32[]{:S(2)}, u32[]{:S(2)}) collective-permute-start(f32[12,512]{0,1:T(8,128)S(1)} %copy.43), channel_id=1, source_target_pairs={{0,8},{8,16},{16,24},{24,0},{32,40},{40,48},{48,56},{56,32},{64,72... | collective-permute-start | bytes 73736 | tf_op jit(solution)/shard_map/ppermute | solution.py:420
  328.3 13.1 %collective-permute-start.12 = (f32[12,512]{0,1:T(8,128)S(1)}, f32[12,512]{0,1:T(8,128)S(1)}, u32[]{:S(2)}, u32[]{:S(2)}) collective-permute-start(f32[12,512]{0,1:T(8,128)S(1)} %copy.43), channel_id=1, source_target_pairs={{0,16},{8,24},{16,0},{24,8},{32,48},{40,56},{48,32},{56,40},{64,80... | collective-permute-start | bytes 73736 | tf_op jit(solution)/shard_map/ppermute | solution.py:420
  330.4 11.0 %collective-permute-start.11 = (f32[12,512]{0,1:T(8,128)S(1)}, f32[12,512]{0,1:T(8,128)S(1)}, u32[]{:S(2)}, u32[]{:S(2)}) collective-permute-start(f32[12,512]{0,1:T(8,128)S(1)} %copy.43), channel_id=1, source_target_pairs={{0,24},{8,0},{16,8},{24,16},{32,56},{40,32},{48,40},{56,48},{64,88... | collective-permute-start | bytes 73736 | tf_op jit(solution)/shard_map/ppermute | solution.py:420

commit v2 on v1

--- a/solution.py
+++ b/solution.py
@@ -17,7 +17,8 @@
 NVIRT = 4
 PAIRS = H // 2
 NEG_FILL = -1e30
-SPLIT = (96, 32)
+SPLIT = (64, 32, 32)
+TOGETHER = (2, 4, 4)
 AXES = ("row", "col")
 F32 = jnp.float32
 BF16 = jnp.bfloat16
@@ -36,23 +37,45 @@
     return partner // grid_cols // blocks_x * mesh_cols + partner % grid_cols // blocks_y
 
 
-def send_kernel(blocks_y, where_to, partners, feats, *refs):
-    nblocks = feats.shape[0]
-    outs, (held, in_sem, out_sems) = refs[: len(SPLIT)], refs[len(SPLIT) :]
-    pltpu.make_async_copy(feats, held, in_sem).start()
-    pltpu.make_async_copy(feats, held, in_sem).wait()
-    first = 0
-    for part, rows in enumerate(SPLIT):
+def send_kernel(first, sides, where_to, partners, feats, *refs):
+    blocks_x, blocks_y = sides
+    nblocks = blocks_x * blocks_y
+    out, *edges = refs[:-3]
+    held, in_sem, out_sem = refs[-3:]
+    rows = out.shape[1]
+    span = pl.ds(0, BLK) if edges else pl.ds(first, rows)
+    loads = [
+        pltpu.make_async_copy(feats.at[block, span], held.at[block, span], in_sem.at[block])
+        for block in range(nblocks)
+    ]
+    for load in loads:
+        load.start()
+    for block, load in enumerate(loads):
+        load.wait()
         for m in range(NEXP):
-            for block in range(nblocks):
-                dest = where_to(partners[block // blocks_y, block % blocks_y, m])
-                pltpu.make_async_copy(
-                    held.at[block, pl.ds(first, rows)], outs[part].at[dest], out_sems.at[part]
-                ).start()
-        first += rows
-    for part in range(len(SPLIT)):
-        every = outs[part].at[pl.ds(0, nblocks * NEXP)]
-        pltpu.make_async_copy(every, every, out_sems.at[part]).wait()
+            dest = where_to(partners[block // blocks_y, block % blocks_y, m])
+            pltpu.make_async_copy(
+                held.at[block, pl.ds(first, rows)], out.at[dest], out_sem.at[0]
+            ).start()
+    if edges:
+        last_row, first_row, last_col, first_col = edges
+        moves = [
+            (held.at[pl.ds(nblocks - blocks_y, blocks_y)], last_row),
+            (held.at[pl.ds(0, blocks_y)], first_row),
+        ]
+        for row in range(blocks_x):
+            moves.append((held.at[row * blocks_y + blocks_y - 1], last_col.at[row]))
+            moves.append((held.at[row * blocks_y], first_col.at[row]))
+        copies = [
+            pltpu.make_async_copy(kept, edge, out_sem.at[1 + index])
+            for index, (kept, edge) in enumerate(moves)
+        ]
+        for copy in copies:
+            copy.start()
+        for copy in copies:
+            copy.wait()
+    every = out.at[pl.ds(0, nblocks * NEXP)]
+    pltpu.make_async_copy(every, every, out_sem.at[0]).wait()
 
 
 def pair_query(query_t, pair):
@@ -156,8 +179,10 @@
                 )
 
 
-def remote_kernel(last, partners, *refs):
-    sources, refs = refs[:NEXP], refs[NEXP:]
+def remote_kernel(last, together, slots, table, *refs):
+    masked = slots != NEXP
+    step = pl.program_id(0)
+    sources, refs = refs[: slots * together], refs[slots * together :]
     query_in, acc_in, top_in, total_in, w_key, w_value_t = refs[:6]
     refs = refs[6:]
     if last:
@@ -168,36 +193,51 @@
     for slot, source in enumerate(sources):
         rows[slot * count : (slot + 1) * count, :] = source[0]
     project_keys(rows, w_key, w_value_t, keys, values_t)
-    query_t = query_in[0]
-    for pair in range(PAIRS):
-        lanes = slice(pair * 2 * HD, (pair + 1) * 2 * HD)
-        query = pair_query(query_t, pair)
-        scores = dot_nn(keys[:, lanes], query)
-        pick = slice(2 * pair, 2 * pair + 1)
-        pick_next = slice(2 * pair + 1, 2 * pair + 2)
-        before = jnp.concatenate([top_in[0, pick, :], top_in[0, pick_next, :]], axis=1)
-        total = jnp.concatenate([total_in[0, pick, :], total_in[0, pick_next, :]], axis=1)
-        top = jnp.maximum(before, jnp.max(scores, axis=0, keepdims=True))
-        fade = jnp.exp(before - top)
-        shares = jnp.exp(scores - top)
-        total = total * fade + jnp.sum(shares, axis=0, keepdims=True)
-        mixed = dot_nn(values_t[lanes, :], shares.astype(BF16))
-        for half, part in enumerate(diagonal(mixed)):
-            head = 2 * pair + half
-            nodes = slice(half * BLK, (half + 1) * BLK)
-            features = slice(head * HD, (head + 1) * HD)
-            gained = acc_in[0, features, :] * fade[:, nodes] + part
-            if last:
-                context[features, :] = (gained / total[:, nodes]).astype(BF16)
-            else:
-                acc_out[0, features, :] = gained
-                top_out[0, head : head + 1, :] = top[:, nodes]
-                total_out[0, head : head + 1, :] = total[:, nodes]
+    for block in range(together):
+        query_t = query_in[block]
+        known = slice(block * slots * count, (block + 1) * slots * count)
+        for pair in range(PAIRS):
+            lanes = slice(pair * 2 * HD, (pair + 1) * 2 * HD)
+            query = pair_query(query_t, pair)
+            scores = dot_nn(keys[known, lanes], query)
+            if masked:
+                alive = [table[slots * (step * together + block) + slot] == 1 for slot in range(slots)]
+                scores = jnp.concatenate(
+                    [
+                        jnp.where(alive[slot], scores[slot * count : (slot + 1) * count], NEG_FILL)
+                        for slot in range(slots)
+                    ],
+                    axis=0,
+                )
+            pick = slice(2 * pair, 2 * pair + 1)
+            pick_next = slice(2 * pair + 1, 2 * pair + 2)
+            before = jnp.concatenate([top_in[block, pick, :], top_in[block, pick_next, :]], axis=1)
+            total = jnp.concatenate(
+                [total_in[block, pick, :], total_in[block, pick_next, :]], axis=1
+            )
+            top = jnp.maximum(before, jnp.max(scores, axis=0, keepdims=True))
+            fade = jnp.exp(before - top)
+            shares = jnp.exp(scores - top)
+            total = total * fade + jnp.sum(shares, axis=0, keepdims=True)
+            mixed = dot_nn(values_t[lanes, known], shares.astype(BF16))
+            for half, part in enumerate(diagonal(mixed)):
+                head = 2 * pair + half
+                nodes = slice(half * BLK, (half + 1) * BLK)
+                features = slice(head * HD, (head + 1) * HD)
+                gained = acc_in[block, features, :] * fade[:, nodes] + part
+                if last:
+                    context[features, block * BLK : (block + 1) * BLK] = (
+                        gained / total[:, nodes]
+                    ).astype(BF16)
+                else:
+                    acc_out[block, features, :] = gained
+                    top_out[block, head : head + 1, :] = top[:, nodes]
+                    total_out[block, head : head + 1, :] = total[:, nodes]
     if last:
         mixed = lax.dot_general(
             context[...], w_out[...], (((0,), (0,)), ((), ())), preferred_element_type=F32
         )
-        node_out[0] = (feats[0].astype(F32) + mixed).astype(BF16)
+        node_out[...] = (feats[...].astype(F32) + mixed.reshape(feats.shape)).astype(BF16)
 
 
 def turn(index, stride, size, shift):
@@ -216,6 +256,23 @@
     return ordered
 
 
+def finish_kernel(*refs):
+    parts, (own, virt_emb, w_out, virt_out, held) = refs[:-5], refs[-5:]
+    size = len(parts)
+    place = lax.rem(lax.axis_index("row"), size)
+    for shift, part in enumerate(parts):
+        held[lax.rem(place + (size - shift), size)] = part[...]
+    every = [held.at[source] for source in range(size)] + [own]
+    top = functools.reduce(jnp.maximum, [one[:NVIRT] for one in every])
+    total, accum = jnp.zeros_like(top), jnp.zeros_like(top)
+    for one in every:
+        fade = jnp.exp(one[:NVIRT] - top)
+        total = total + one[NVIRT : 2 * NVIRT] * fade
+        accum = accum + one[2 * NVIRT :] * fade
+    context = (accum / total).astype(BF16)
+    virt_out[...] = virt_emb[...].astype(F32) + dot_nn(context, w_out[...])
+
+
 def merge(parts):
     tops = [part[:NVIRT] for part in parts]
     top = functools.reduce(jnp.maximum, tops)
@@ -227,7 +284,7 @@
     return jnp.concatenate([top, *sums], axis=0)
 
 
-def halo(feats):
+def halo(last_row, first_row, last_col, first_col):
     count_x, count_y = lax.axis_size("row"), lax.axis_size("col")
 
     def shift(edge, axis, count, step):
@@ -235,10 +292,10 @@
         return lax.ppermute(edge, axis, pairs)
 
     return (
-        shift(feats[-1], "row", count_x, 1),
-        shift(feats[0], "row", count_x, -1),
-        shift(feats[:, -1], "col", count_y, 1),
-        shift(feats[:, 0], "col", count_y, -1),
+        shift(last_row, "row", count_x, 1),
+        shift(first_row, "row", count_x, -1),
+        shift(last_col, "col", count_y, 1),
+        shift(first_col, "col", count_y, -1),
     )
 
 
@@ -254,20 +311,27 @@
     shapes = jax.ShapeDtypeStruct
     anywhere = pl.BlockSpec(memory_space=pl.ANY)
 
-    edges = halo(feats)
-    outgoing = pl.pallas_call(
-        functools.partial(send_kernel, blocks_y, where_to),
-        name="send",
-        out_shape=[shapes((devices, rows, D), BF16) for rows in SPLIT],
-        in_specs=[pl.BlockSpec(memory_space=pltpu.SMEM), anywhere],
-        out_specs=[anywhere] * len(SPLIT),
-        scratch_shapes=[
-            pltpu.VMEM((nblocks, BLK, D), BF16),
-            pltpu.SemaphoreType.DMA,
-            pltpu.SemaphoreType.DMA((len(SPLIT),)),
-        ],
-        cost_estimate=pl.CostEstimate(flops=0, bytes_accessed=10 << 20, transcendentals=0),
-    )(partners, flat)
+    outgoing = []
+    first = 0
+    for part, rows in enumerate(SPLIT):
+        sides = () if part else (blocks_y, blocks_y, blocks_x, blocks_x)
+        out_shape = [shapes((devices, rows, D), BF16), *(shapes((n, BLK, D), BF16) for n in sides)]
+        slots, *edges = pl.pallas_call(
+            functools.partial(send_kernel, first, (blocks_x, blocks_y), where_to),
+            out_shape=out_shape,
+            in_specs=[pl.BlockSpec(memory_space=pltpu.SMEM), anywhere],
+            out_specs=[anywhere] * len(out_shape),
+            scratch_shapes=[
+                pltpu.VMEM((nblocks, BLK, D), BF16),
+                pltpu.SemaphoreType.DMA((nblocks,)),
+                pltpu.SemaphoreType.DMA((3 + 2 * blocks_x,)),
+            ],
+            cost_estimate=pl.CostEstimate(flops=0, bytes_accessed=10 << 20, transcendentals=0),
+        )(partners, flat)
+        outgoing.append(slots)
+        first += rows
+        if edges:
+            edges_in = halo(*edges)
     arrived = []
     for part, slots in enumerate(outgoing):
         arrived.append(lax.all_to_all(slots, AXES, split_axis=0, concat_axis=0, tiled=True))
@@ -298,26 +362,24 @@
         ],
         axis=-1,
     )
-    live = ((link_mask == 1) & inside).astype(jnp.int32)
-
-    padded = jnp.concatenate([flat, *edges], axis=0)
-    start_up = nblocks
-    start_down = start_up + blocks_y
-    start_left = start_down + blocks_y
-    start_right = start_left + blocks_x
+    live = (link_mask == 1) & inside
+    at_x, at_y = jnp.arange(blocks_x)[:, None], jnp.arange(blocks_y)[None, :]
+    outer = (at_x == 0, at_x == blocks_x - 1, at_y == 0, at_y == blocks_y - 1)
+    far = jnp.stack([jnp.broadcast_to(side, (blocks_x, blocks_y)) for side in outer], axis=-1)
+    near_live = (live & ~far).astype(jnp.int32)
+    far_live = (live & far).reshape(nblocks, 2, 2).any(axis=-1).astype(jnp.int32).reshape(-1)
 
     def above(b, *_):
-        return (jnp.where(b < blocks_y, start_up + b, b - blocks_y), 0, 0)
+        return (jnp.where(b < blocks_y, b, b - blocks_y), 0, 0)
 
     def below(b, *_):
-        near = b - (nblocks - blocks_y)
-        return (jnp.where(near >= 0, start_down + near, b + blocks_y), 0, 0)
+        return (jnp.where(b >= nblocks - blocks_y, b, b + blocks_y), 0, 0)
 
     def before(b, *_):
-        return (jnp.where(b % blocks_y == 0, start_left + b // blocks_y, b - 1), 0, 0)
+        return (jnp.where(b % blocks_y == 0, b, b - 1), 0, 0)
 
     def after(b, *_):
-        return (jnp.where(b % blocks_y == blocks_y - 1, start_right + b // blocks_y, b + 1), 0, 0)
+        return (jnp.where(b % blocks_y == blocks_y - 1, b, b + 1), 0, 0)
 
     def same(b, *_):
         return (b, 0, 0)
@@ -361,70 +423,93 @@
             flops=40_000_000_000, bytes_accessed=30 << 20, transcendentals=nblocks * H * BLK * local_keys
         ),
     )(
-        live, padded, padded, padded, padded, padded, virt_ids.reshape(nblocks, 1, BLK),
+        near_live, flat, flat, flat, flat, flat, virt_ids.reshape(nblocks, 1, BLK),
         w_query_t, w_key, w_value_t, virt_key_rows, virt_value_cols, virt_query_rows,
     )
 
-    def partner_block(m):
-        def index(b, partner):
-            return (where_to(partner[b // blocks_y, b % blocks_y, m]), 0, 0)
-
-        return index
-
-    node_out = None
-    for part, rows in enumerate(SPLIT):
-        last = part == len(SPLIT) - 1
+    def add_keys(source, rows, together, slots, table, index, state, finish=()):
+        def blocks_of(*shape):
+            return pl.BlockSpec((together, *shape), same)
+
+        states = [blocks_of(D, BLK), blocks_of(H, BLK), blocks_of(H, BLK)]
         in_specs = [
-            *(pl.BlockSpec((1, rows, D), partner_block(m)) for m in range(NEXP)),
-            pl.BlockSpec(turned, same), *state_specs, weight, weight,
+            *(
+                pl.BlockSpec((1, rows, D), functools.partial(index, together, offset, slot))
+                for offset in range(together)
+                for slot in range(slots)
+            ),
+            blocks_of(D, BLK), *states, weight, weight,
         ]
-        operands = [*[arrived[part]] * NEXP, query_t, *state, w_key, w_value_t]
+        count = together * slots * rows
         scratch = [
-            pltpu.VMEM((NEXP * rows, D), BF16),
-            pltpu.VMEM((NEXP * rows, D), BF16),
-            pltpu.VMEM((D, NEXP * rows), BF16),
+            pltpu.VMEM((count, D), BF16), pltpu.VMEM((count, D), BF16), pltpu.VMEM((D, count), BF16)
         ]
-        if last:
-            in_specs += [pl.BlockSpec(block, same), weight]
-            operands += [flat, w_out]
-            out_shape, out_specs = shapes(flat.shape, BF16), pl.BlockSpec(block, same)
-            scratch += [pltpu.VMEM((D, BLK), BF16)]
+        if finish:
+            in_specs += [blocks_of(BLK, D), weight]
+            out_shape, out_specs = shapes(flat.shape, BF16), blocks_of(BLK, D)
+            scratch += [pltpu.VMEM((D, together * BLK), BF16)]
         else:
-            out_shape, out_specs = state_shapes, state_specs
-        result = pl.pallas_call(
-            functools.partial(remote_kernel, last),
+            out_shape, out_specs = state_shapes, states
+        return pl.pallas_call(
+            functools.partial(remote_kernel, bool(finish), together, slots),
             out_shape=out_shape,
             grid_spec=pltpu.PrefetchScalarGridSpec(
-                num_scalar_prefetch=1, grid=(nblocks,), in_specs=in_specs, out_specs=out_specs,
-                scratch_shapes=scratch,
+                num_scalar_prefetch=1, grid=(nblocks // together,), in_specs=in_specs,
+                out_specs=out_specs, scratch_shapes=scratch,
             ),
             cost_estimate=pl.CostEstimate(
-                flops=25_000_000_000 * rows // BLK,
+                flops=50_000_000 * slots * rows,
                 bytes_accessed=20 << 20,
-                transcendentals=nblocks * H * BLK * NEXP * rows,
+                transcendentals=nblocks * H * BLK * slots * rows,
             ),
-        )(partners, *operands)
-        if last:
-            node_out = result
-        else:
-            state = result
+        )(table, *[source] * (slots * together), query_t, *state, w_key, w_value_t, *finish)
+
+    def partner_block(together, offset, slot, b, partner):
+        at = b * together + offset
+        return (where_to(partner[at // blocks_y, at % blocks_y, slot]), 0, 0)
+
+    def edge_block(together, offset, slot, b, _):
+        at = b * together + offset
+        row, col = at // blocks_y, at % blocks_y
+        if slot == 0:
+            return (jnp.where(row == blocks_x - 1, blocks_y + col, col), 0, 0)
+        return (2 * blocks_y + jnp.where(col == blocks_y - 1, blocks_x + row, row), 0, 0)
+
+    state = add_keys(arrived[0], SPLIT[0], TOGETHER[0], NEXP, partners, partner_block, state)
+    edge_blocks = jnp.concatenate(edges_in, axis=0)
+    state = add_keys(edge_blocks, BLK, TOGETHER[0], 2, far_live, edge_block, state)
+    state = add_keys(arrived[1], SPLIT[1], TOGETHER[1], NEXP, partners, partner_block, state)
+    node_out = add_keys(
+        arrived[2], SPLIT[2], TOGETHER[2], NEXP, partners, partner_block, state,
+        (flat, w_out),
+    )
 
     own_score = (
         jnp.sum((virt_query.astype(F32) * virt_key.astype(F32)).reshape(NVIRT, H, HD), axis=-1) * scale
     )
     own_score = jnp.repeat(own_score, HD, axis=1)
     part = virt_part
-    ways = (("col", mesh_cols, 1, 2), ("col", mesh_cols, 2, 4), ("row", mesh_rows, 4, 4), ("row", mesh_rows, 1, 4))
-    for axis, count, stride, size in ways:
-        others = [
+    ways = (
+        ("col", mesh_cols, 1, 2),
+        ("col", mesh_cols, 2, mesh_cols // 2),
+        ("row", mesh_rows, 4, mesh_rows // 4),
+        ("row", mesh_rows, 1, 4),
+    )
+    for stage, (axis, count, stride, size) in enumerate(ways):
+        parts = [part] + [
             lax.ppermute(part, axis, [(i, turn(i, stride, size, shift)) for i in range(count)])
             for shift in range(1, size)
         ]
-        part = merge(in_order([part, *others], lax.axis_index(axis) // stride % size))
+        if stage < len(ways) - 1:
+            part = merge(in_order(parts, lax.axis_index(axis) // stride % size))
     own = jnp.concatenate([own_score, jnp.ones_like(own_score), virt_value.astype(F32)], axis=0)
-    part = merge([part, own])
-    virt_context = (part[2 * NVIRT :] / part[NVIRT : 2 * NVIRT]).astype(BF16)
-    virt_out = virt_emb.astype(F32) + jnp.dot(virt_context, w_out, preferred_element_type=F32)
+    virt_out = pl.pallas_call(
+        finish_kernel,
+        name="finish",
+        out_shape=shapes((NVIRT, D), F32),
+        scratch_shapes=[pltpu.VMEM((len(parts), 3 * NVIRT, D), F32)],
+        cost_estimate=pl.CostEstimate(flops=1 << 21, bytes_accessed=1 << 20, transcendentals=1 << 16),
+    )(*parts, own, virt_emb, w_out)
     return node_out.reshape(feats.shape), virt_out
 
 

time: 419 us -> 358 us (0.85)
  the two profiles are of different devices: /device:TPU:1 before, /device:TPU:14 now
where the time goes in v2:
time: 358 us; the launch traced here: 357 us
  Pallas kernels  163 us (46%)
  waiting for transfers between devices  124 us (35%)
  starting transfers between devices  57.8 us (16%)
  local copies, waits for them, and re-layouts  5.95 us (2%)
  other arithmetic  4.89 us (1%)
    pallas_call x4, Pallas kernels, add_keys(): pl.pallas_call(functools.partial(remote_kernel, bool(finish), together, s...  88.9 us
    ppermute x10, waiting for transfers between devices, shards(): lax.ppermute(part, axis, [(i, turn(i, stride, size, shift)) for i in rang...  79.9 us
    pallas_call x1, Pallas kernels, shards(): pl.pallas_call(local_kernel, name='local', out_shape=[shapes((nblocks, D,...  60.7 us
    all_to_all x3, waiting for transfers between devices, shards(): lax.all_to_all(slots, AXES, split_axis=0, concat_axis=0, tiled=True)  44 us
    all_to_all x3, starting transfers between devices, shards(): lax.all_to_all(slots, AXES, split_axis=0, concat_axis=0, tiled=True)  28.8 us
    ppermute x10, starting transfers between devices, shards(): lax.ppermute(part, axis, [(i, turn(i, stride, size, shift)) for i in rang...  15.5 us
    ppermute x4, starting transfers between devices, shift(): return lax.ppermute(edge, axis, pairs)  13.5 us
    pallas_call x3, Pallas kernels, shards(): pl.pallas_call(functools.partial(send_kernel, first, (blocks_x, blocks_y)...  11.4 us
  transfers between devices with their start and end apart: 17, of which 6 were waited for; matrix products, arithmetic and copies ran while one was open for 3% of the time, Pallas kernels for 40%

profile of v2, /device:TPU:14, one launch (start us, length us, event | category | flops | bytes accessed | tf_op | source)
XLA Modules:
  0.0 357.2 jit_solution(13050112374116422067)
XLA Ops:
  0.6 3.3 shard_map.105
  3.9 10.9 %all-to-all-start.1 = ((bf16[128,32,512]{2,1,0:T(8,128)(2,1)}), bf16[128,32,512]{2,1,0:T(8,128)(2,1)}, u32[]{:S(2)}, u32[]{:S(2)}) async-start(bf16[128,32,512]{2,1,0:T(8,128)(2,1)} %shard_map.105), calls=%async_computation.1 | async-start | bytes 8388608 | tf_op jit(solution)/shard_map/all_to_all | solution.py:337
  14.8 4.7 %shard_map.106 = (bf16[128,64,512]{2,1,0:T(8,128)(2,1)}, bf16[4,128,512]{2,1,0:T(8,128)(2,1)}, bf16[4,128,512]{2,1,0:T(8,128)(2,1)}, bf16[4,128,512]{2,1,0:T(8,128)(2,1)}, bf16[4,128,512]{2,1,0:T(8,128)(2,1)}) custom-call(s32[4,4,4]{2,1,0:T(4,128)} %table.5, bf16[16,128,512]{2,1,0:T(8,128)(2,1)} %bitcast.15), custom_call_target="tpu_custom_call" | custom-call | bytes 10485760 | tf_op jit(solution)/shard_map/pallas_call | solution.py:319
  21.6 44.0 %all-to-all-done.1.refs_0_.refs_1_.refs_2_.refs_3_.refs_4_.refs_5_.refs_6_.refs_7_.refs_8_.refs_9_.refs_10_.refs_11_.refs_12_.refs_13_.refs_14_.refs_15_ = bf16[128,32,512]{2,1,0:T(8,128)(2,1)} async-done(((bf16[128,32,512]{2,1,0:T(8,128)(2,1)}), bf16[128,32,512]{2,1,0:T(8,128)(2,1)}, u32[]{:S(2)}, u32[]{:S(2)}) %all-to-all-start.1) | async-done | bytes 4194336 | tf_op jit(solution)/shard_map/all_to_all | solution.py:337
  65.6 7.6 %all-to-all-start.2 = ((bf16[128,64,512]{2,1,0:T(8,128)(2,1)}), bf16[128,64,512]{2,1,0:T(8,128)(2,1)}, u32[]{:S(2)}, u32[]{:S(2)}) async-start(bf16[128,64,512]{2,1,0:T(8,128)(2,1)} %get-tuple-element.26), calls=%async_computation.2 | async-start | bytes 16777216 | tf_op jit(solution)/shard_map/all_to_all | solution.py:337
  77.1 60.7 %local.1 = (bf16[16,512,128]{2,1,0:T(8,128)(2,1)}, f32[16,512,128]{2,1,0:T(8,128)}, f32[16,8,128]{2,1,0:T(8,128)}, f32[16,8,128]{2,1,0:T(8,128)}, f32[12,512]{1,0:T(8,128)}) custom-call(s32[4,4,4]{2,1,0:T(4,128)} %and_convert_fusion.live, bf16[16,128,512]{2,1,0:T(8,128)(2,1)} %bitcast.16, bf16[16,128,512]{2,1,0:T(8,128)(2,1)} %bitcast.17, ...), custom_call_target="tpu_custom_call" | custom-call | flops 40000000000 | bytes 31457280 | tf_op jit(solution)/shard_map/local/pallas_call | solution.py:399
  142.2 2.1 collective-permute-start.7
  144.3 29.1 %collective-permute-done.5 = f32[12,512]{1,0:T(8,128)S(1)} collective-permute-done((f32[12,512]{1,0:T(8,128)S(1)}, f32[12,512]{1,0:T(8,128)S(1)}, u32[]{:S(2)}, u32[]{:S(2)}) %collective-permute-start.5) | collective-permute-done | bytes 24608 | tf_op jit(solution)/shard_map/ppermute | solution.py:500
  173.9 2.0 collective-permute-start.8
  175.9 1.8 collective-permute-start.9
  177.7 2.9 collective-permute-start
  180.6 5.0 %collective-permute-start.1 = (bf16[4,128,512]{2,1,0:T(8,128)(2,1)}, bf16[4,128,512]{2,1,0:T(8,128)(2,1)S(1)}, u32[]{:S(2)}, u32[]{:S(2)}) collective-permute-start(bf16[4,128,512]{2,1,0:T(8,128)(2,1)} %get-tuple-element.23), channel_id=1, source_target_pairs={{8,0},{16,8},{24,16},{32,24},{40,32},{48,40},{56,48},{64,56},{72,6... | collective-permute-start | bytes 1572872 | tf_op jit(solution)/shard_map/ppermute | solution.py:292
  185.8 3.4 shard_map.104
  189.2 1.9 collective-permute-start.2
  191.2 3.6 %collective-permute-start.3 = (bf16[4,128,512]{2,1,0:T(8,128)(2,1)S(1)}, bf16[4,128,512]{2,1,0:T(8,128)(2,1)S(1)}, u32[]{:S(2)}, u32[]{:S(2)}) collective-permute-start(bf16[4,128,512]{2,1,0:T(8,128)(2,1)S(1)} %copy-done.9), channel_id=1, source_target_pairs={{1,0},{2,1},{3,2},{4,3},{5,4},{6,5},{7,6},{9,8},{10,9},{11,10},{12... | collective-permute-start | bytes 1572872 | tf_op jit(solution)/shard_map/ppermute | solution.py:292
  194.9 10.3 %all-to-all-start = ((bf16[128,32,512]{2,1,0:T(8,128)(2,1)}), bf16[128,32,512]{2,1,0:T(8,128)(2,1)}, u32[]{:S(2)}, u32[]{:S(2)}) async-start(bf16[128,32,512]{2,1,0:T(8,128)(2,1)} %shard_map.104), calls=%async_computation | async-start | bytes 8388608 | tf_op jit(solution)/shard_map/all_to_all | solution.py:337
  207.3 42.9 %collective-permute-done.11.refs_1_ = f32[12,512]{1,0:T(8,128)S(1)} collective-permute-done((f32[12,512]{1,0:T(8,128)S(1)}, f32[12,512]{1,0:T(8,128)S(1)}, u32[]{:S(2)}, u32[]{:S(2)}) %collective-permute-start.11) | collective-permute-done | bytes 24608 | tf_op jit(solution)/shard_map/ppermute | solution.py:500
  250.4 6.3 %collective-permute-done.12.refs_2_ = f32[12,512]{1,0:T(8,128)S(1)} collective-permute-done((f32[12,512]{1,0:T(8,128)S(1)}, f32[12,512]{1,0:T(8,128)S(1)}, u32[]{:S(2)}, u32[]{:S(2)}) %collective-permute-start.12) | collective-permute-done | bytes 24608 | tf_op jit(solution)/shard_map/ppermute | solution.py:500
  256.7 5.5 %collective-permute-start.13 = (f32[12,512]{1,0:T(8,128)S(1)}, f32[12,512]{1,0:T(8,128)S(1)}, u32[]{:S(2)}, u32[]{:S(2)}) collective-permute-start(f32[12,512]{1,0:T(8,128)S(1)} %pad_maximum_fusion.3.refs_0_), channel_id=1, source_target_pairs={{0,24},{8,0},{16,8},{24,16},{32,56},{40,32},{48,40},{56,48},{64,88... | collective-permute-start | bytes 73736 | tf_op jit(solution)/shard_map/ppermute | solution.py:500
  264.6 2.0 finish.1
  268.1 31.7 %shard_map.107 = (f32[16,512,128]{2,1,0:T(8,128)}, f32[16,8,128]{2,1,0:T(8,128)}, f32[16,8,128]{2,1,0:T(8,128)}) custom-call(s32[4,4,4]{2,1,0:T(4,128)} %table.5, bf16[128,64,512]{2,1,0:T(8,128)(2,1)} %all-to-all-done.2.refs_0_.refs_1_.refs_2_.refs_3_.refs_4_.refs_5_.refs_6_.refs_7_, ...), custom_call_target="tpu_custom_call" | custom-call | flops 12800000000 | bytes 20971520 | tf_op jit(solution)/shard_map/pallas_call | solution.py:453
  299.8 28.3 %shard_map.108 = (f32[16,512,128]{2,1,0:T(8,128)}, f32[16,8,128]{2,1,0:T(8,128)}, f32[16,8,128]{2,1,0:T(8,128)}) custom-call(s32[32]{0:T(128)} %reshape.132.table, bf16[16,128,512]{2,1,0:T(8,128)(2,1)} %pad_maximum_fusion.refs_0_.refs_1_.refs_2_.refs_3_, bf16[16,128,512]{2,1,0:T(8,128)(2,1)} %pad_maximum_fusion.refs_0_.refs_1_.refs_2_.refs_3_, ...), custom_call_target="tpu_custom_call" | custom-call | flops 12800000000 | bytes 20971520 | tf_op jit(solution)/shard_map/pallas_call | solution.py:453
  328.1 13.8 %shard_map.109 = (f32[16,512,128]{2,1,0:T(8,128)}, f32[16,8,128]{2,1,0:T(8,128)}, f32[16,8,128]{2,1,0:T(8,128)}) custom-call(s32[4,4,4]{2,1,0:T(4,128)} %table.5, bf16[128,32,512]{2,1,0:T(8,128)(2,1)} %all-to-all-done.1.refs_0_.refs_1_.refs_2_.refs_3_.refs_4_.refs_5_.refs_6_.refs_7_.refs_8_.refs_9_.refs_10_.refs_11_.refs_12_.refs_13_.refs_14_.refs_15_, ...), custom_call_target="tpu_custom_call" | custom-call | flops 6400000000 | bytes 20971520 | tf_op jit(solution)/shard_map/pallas_call | solution.py:453
  342.0 15.1 %shard_map.110 = bf16[16,128,512]{2,1,0:T(8,128)(2,1)} custom-call(s32[4,4,4]{2,1,0:T(4,128)} %table.5, bf16[128,32,512]{2,1,0:T(8,128)(2,1)} %all-to-all-done.refs_0_.refs_1_.refs_2_.refs_3_.refs_4_.refs_5_.refs_6_.refs_7_.refs_8_.refs_9_.refs_10_.refs_11_.refs_12_.refs_13_.refs_14_.refs_15_, ...), custom_call_target="tpu_custom_call" | custom-call | flops 6400000000 | bytes 20971520 | tf_op jit(solution)/shard_map/pallas_call | solution.py:453
  (95 shorter events, 16.9 us)
Async XLA Ops:
  3.9 61.6 %all-to-all-start.1 = ((bf16[128,32,512]{2,1,0:T(8,128)(2,1)}), bf16[128,32,512]{2,1,0:T(8,128)(2,1)}, u32[]{:S(2)}, u32[]{:S(2)}) async-start(bf16[128,32,512]{2,1,0:T(8,128)(2,1)} %shard_map.105), calls=%async_computation.1 | async-start | bytes 8388608 | tf_op jit(solution)/shard_map/all_to_all | solution.py:337
  14.8 5.8 %copy-start.1 = (bf16[512,512]{1,0:T(8,128)(2,1)S(1)}, bf16[512,512]{1,0:T(8,128)(2,1)}, u32[]{:S(2)}) copy-start(bf16[512,512]{1,0:T(8,128)(2,1)} %param.11) | copy-start | bytes 1572868
  65.6 7.7 %copy-start = (bf16[512,512]{1,0:T(8,128)(2,1)S(1)}, bf16[512,512]{1,0:T(8,128)(2,1)}, u32[]{:S(2)}) copy-start(bf16[512,512]{1,0:T(8,128)(2,1)} %refs_20_.3) | copy-start | bytes 1572868
  65.6 7.7 %copy-start.8 = (bf16[4,512]{1,0:T(4,128)(2,1)S(1)}, bf16[4,512]{1,0:T(4,128)(2,1)}, u32[]{:S(2)}) copy-start(bf16[4,512]{1,0:T(4,128)(2,1)} %refs_5_.1) | copy-start | bytes 12292
  65.6 129.4 %all-to-all-start.2 = ((bf16[128,64,512]{2,1,0:T(8,128)(2,1)}), bf16[128,64,512]{2,1,0:T(8,128)(2,1)}, u32[]{:S(2)}, u32[]{:S(2)}) async-start(bf16[128,64,512]{2,1,0:T(8,128)(2,1)} %get-tuple-element.26), calls=%async_computation.2 | async-start | bytes 16777216 | tf_op jit(solution)/shard_map/all_to_all | solution.py:337
  137.8 1.5 collective-permute-start.4
  140.1 33.2 %collective-permute-start.5 = (f32[12,512]{1,0:T(8,128)S(1)}, f32[12,512]{1,0:T(8,128)S(1)}, u32[]{:S(2)}, u32[]{:S(2)}) collective-permute-start(f32[12,512]{1,0:T(8,128)S(1)} %pad_maximum_fusion.1), channel_id=1, source_target_pairs={{0,6},{1,7},{2,0},{3,1},{4,2},{5,3},{6,4},{7,5},{8,14},{9,15},{10,... | collective-permute-start | bytes 73736 | tf_op jit(solution)/shard_map/ppermute | solution.py:500
  141.0 32.7 %collective-permute-start.6 = (f32[12,512]{1,0:T(8,128)S(1)}, f32[12,512]{1,0:T(8,128)S(1)}, u32[]{:S(2)}, u32[]{:S(2)}) collective-permute-start(f32[12,512]{1,0:T(8,128)S(1)} %pad_maximum_fusion.1), channel_id=1, source_target_pairs={{0,4},{1,5},{2,6},{3,7},{4,0},{5,1},{6,2},{7,3},{8,12},{9,13},{10,... | collective-permute-start | bytes 73736 | tf_op jit(solution)/shard_map/ppermute | solution.py:500
  142.2 31.5 %collective-permute-start.7 = (f32[12,512]{1,0:T(8,128)S(1)}, f32[12,512]{1,0:T(8,128)S(1)}, u32[]{:S(2)}, u32[]{:S(2)}) collective-permute-start(f32[12,512]{1,0:T(8,128)S(1)} %pad_maximum_fusion.1), channel_id=1, source_target_pairs={{0,2},{1,3},{2,4},{3,5},{4,6},{5,7},{6,0},{7,1},{8,10},{9,11},{10,... | collective-permute-start | bytes 73736 | tf_op jit(solution)/shard_map/ppermute | solution.py:500
  173.8 15.4 %collective-permute-start.10 = (f32[12,512]{1,0:T(8,128)S(1)}, f32[12,512]{1,0:T(8,128)S(1)}, u32[]{:S(2)}, u32[]{:S(2)}) collective-permute-start(f32[12,512]{1,0:T(8,128)S(1)} %pad_maximum_fusion.2), channel_id=1, source_target_pairs={{0,32},{8,40},{16,48},{24,56},{32,64},{40,72},{48,80},{56,88},{64,... | collective-permute-start | bytes 73736 | tf_op jit(solution)/shard_map/ppermute | solution.py:500
  173.9 17.2 %collective-permute-start.8 = (f32[12,512]{1,0:T(8,128)S(1)}, f32[12,512]{1,0:T(8,128)S(1)}, u32[]{:S(2)}, u32[]{:S(2)}) collective-permute-start(f32[12,512]{1,0:T(8,128)S(1)} %pad_maximum_fusion.2), channel_id=1, source_target_pairs={{0,96},{8,104},{16,112},{24,120},{32,0},{40,8},{48,16},{56,24},{64... | collective-permute-start | bytes 73736 | tf_op jit(solution)/shard_map/ppermute | solution.py:500
  175.9 18.9 %collective-permute-start.9 = (f32[12,512]{1,0:T(8,128)S(1)}, f32[12,512]{1,0:T(8,128)S(1)}, u32[]{:S(2)}, u32[]{:S(2)}) collective-permute-start(f32[12,512]{1,0:T(8,128)S(1)} %pad_maximum_fusion.2), channel_id=1, source_target_pairs={{0,64},{8,72},{16,80},{24,88},{32,96},{40,104},{48,112},{56,120},{... | collective-permute-start | bytes 73736 | tf_op jit(solution)/shard_map/ppermute | solution.py:500
  177.7 88.8 %collective-permute-start = (bf16[4,128,512]{2,1,0:T(8,128)(2,1)}, bf16[4,128,512]{2,1,0:T(8,128)(2,1)S(1)}, u32[]{:S(2)}, u32[]{:S(2)}) collective-permute-start(bf16[4,128,512]{2,1,0:T(8,128)(2,1)} %get-tuple-element.22), channel_id=1, source_target_pairs={{0,8},{8,16},{16,24},{24,32},{32,40},{40,48},{48,56},{56,64},{64,7... | collective-permute-start | bytes 1572872 | tf_op jit(solution)/shard_map/ppermute | solution.py:292
  180.6 85.9 %collective-permute-start.1 = (bf16[4,128,512]{2,1,0:T(8,128)(2,1)}, bf16[4,128,512]{2,1,0:T(8,128)(2,1)S(1)}, u32[]{:S(2)}, u32[]{:S(2)}) collective-permute-start(bf16[4,128,512]{2,1,0:T(8,128)(2,1)} %get-tuple-element.23), channel_id=1, source_target_pairs={{8,0},{16,8},{24,16},{32,24},{40,32},{48,40},{56,48},{64,56},{72,6... | collective-permute-start | bytes 1572872 | tf_op jit(solution)/shard_map/ppermute | solution.py:292
  185.8 5.4 %copy-start.9 = (bf16[4,128,512]{2,1,0:T(8,128)(2,1)S(1)}, bf16[4,128,512]{2,1,0:T(8,128)(2,1)}, u32[]{:S(2)}) copy-start(bf16[4,128,512]{2,1,0:T(8,128)(2,1)} %get-tuple-element.25) | copy-start | bytes 1572868
  189.2 77.3 %collective-permute-start.2 = (bf16[4,128,512]{2,1,0:T(8,128)(2,1)S(1)}, bf16[4,128,512]{2,1,0:T(8,128)(2,1)S(1)}, u32[]{:S(2)}, u32[]{:S(2)}) collective-permute-start(bf16[4,128,512]{2,1,0:T(8,128)(2,1)S(1)} %copy-done.10), channel_id=1, source_target_pairs={{0,1},{1,2},{2,3},{3,4},{4,5},{5,6},{6,7},{8,9},{9,10},{10,11},{11... | collective-permute-start | bytes 1572872 | tf_op jit(solution)/shard_map/ppermute | solution.py:292
  191.2 75.4 %collective-permute-start.3 = (bf16[4,128,512]{2,1,0:T(8,128)(2,1)S(1)}, bf16[4,128,512]{2,1,0:T(8,128)(2,1)S(1)}, u32[]{:S(2)}, u32[]{:S(2)}) collective-permute-start(bf16[4,128,512]{2,1,0:T(8,128)(2,1)S(1)} %copy-done.9), channel_id=1, source_target_pairs={{1,0},{2,1},{3,2},{4,3},{5,4},{6,5},{7,6},{9,8},{10,9},{11,10},{12... | collective-permute-start | bytes 1572872 | tf_op jit(solution)/shard_map/ppermute | solution.py:292
  194.9 147.0 %all-to-all-start = ((bf16[128,32,512]{2,1,0:T(8,128)(2,1)}), bf16[128,32,512]{2,1,0:T(8,128)(2,1)}, u32[]{:S(2)}, u32[]{:S(2)}) async-start(bf16[128,32,512]{2,1,0:T(8,128)(2,1)} %shard_map.104), calls=%async_computation | async-start | bytes 8388608 | tf_op jit(solution)/shard_map/all_to_all | solution.py:337
  205.3 58.6 %copy-start.3 = (f32[12,512]{1,0:T(8,128)}, f32[12,512]{1,0:T(8,128)S(1)}, u32[]{:S(2)}) copy-start(f32[12,512]{1,0:T(8,128)S(1)} %pad_maximum_fusion.3.refs_0_) | copy-start | bytes 73732
  205.3 44.8 %collective-permute-start.11 = (f32[12,512]{1,0:T(8,128)S(1)}, f32[12,512]{1,0:T(8,128)S(1)}, u32[]{:S(2)}, u32[]{:S(2)}) collective-permute-start(f32[12,512]{1,0:T(8,128)S(1)} %pad_maximum_fusion.3.refs_0_), channel_id=1, source_target_pairs={{0,8},{8,16},{16,24},{24,0},{32,40},{40,48},{48,56},{56,32},{64,72... | collective-permute-start | bytes 73736 | tf_op jit(solution)/shard_map/ppermute | solution.py:500
  250.2 13.8 %copy-start.4 = (f32[12,512]{1,0:T(8,128)}, f32[12,512]{1,0:T(8,128)S(1)}, u32[]{:S(2)}) copy-start(f32[12,512]{1,0:T(8,128)S(1)} %collective-permute-done.11.refs_1_) | copy-start | bytes 73732
  250.2 6.5 %collective-permute-start.12 = (f32[12,512]{1,0:T(8,128)S(1)}, f32[12,512]{1,0:T(8,128)S(1)}, u32[]{:S(2)}, u32[]{:S(2)}) collective-permute-start(f32[12,512]{1,0:T(8,128)S(1)} %pad_maximum_fusion.3.refs_0_), channel_id=1, source_target_pairs={{0,16},{8,24},{16,0},{24,8},{32,48},{40,56},{48,32},{56,40},{64,80... | collective-permute-start | bytes 73736 | tf_op jit(solution)/shard_map/ppermute | solution.py:500
  256.7 7.2 %copy-start.5 = (f32[12,512]{1,0:T(8,128)}, f32[12,512]{1,0:T(8,128)S(1)}, u32[]{:S(2)}) copy-start(f32[12,512]{1,0:T(8,128)S(1)} %collective-permute-done.12.refs_2_) | copy-start | bytes 73732
  256.7 7.2 %collective-permute-start.13 = (f32[12,512]{1,0:T(8,128)S(1)}, f32[12,512]{1,0:T(8,128)S(1)}, u32[]{:S(2)}, u32[]{:S(2)}) collective-permute-start(f32[12,512]{1,0:T(8,128)S(1)} %pad_maximum_fusion.3.refs_0_), channel_id=1, source_target_pairs={{0,24},{8,0},{16,8},{24,16},{32,56},{40,32},{48,40},{56,48},{64,88... | collective-permute-start | bytes 73736 | tf_op jit(solution)/shard_map/ppermute | solution.py:500
  (4 other events, 11.3 us)

commit v3 on v2

--- a/solution.py
+++ b/solution.py
@@ -43,9 +43,8 @@
     out, *edges = refs[:-3]
     held, in_sem, out_sem = refs[-3:]
     rows = out.shape[1]
-    span = pl.ds(0, BLK) if edges else pl.ds(first, rows)
     loads = [
-        pltpu.make_async_copy(feats.at[block, span], held.at[block, span], in_sem.at[block])
+        pltpu.make_async_copy(feats.at[block], held.at[block], in_sem.at[block])
         for block in range(nblocks)
     ]
     for load in loads:
@@ -314,7 +313,7 @@
     outgoing = []
     first = 0
     for part, rows in enumerate(SPLIT):
-        sides = () if part else (blocks_y, blocks_y, blocks_x, blocks_x)
+        sides = (blocks_y, blocks_y, blocks_x, blocks_x) if part == 1 else ()
         out_shape = [shapes((devices, rows, D), BF16), *(shapes((n, BLK, D), BF16) for n in sides)]
         slots, *edges = pl.pallas_call(
             functools.partial(send_kernel, first, (blocks_x, blocks_y), where_to),

time: 358 us -> 359 us (level)
  no operation moved by 1% of the time
where the time goes in v3:
time: 359 us; the launch traced here: 358 us
  Pallas kernels  163 us (45%)
  waiting for transfers between devices  125 us (35%)
  starting transfers between devices  57.6 us (16%)
  local copies, waits for them, and re-layouts  5.95 us (2%)
  other arithmetic  4.89 us (1%)
    pallas_call x4, Pallas kernels, add_keys(): pl.pallas_call(functools.partial(remote_kernel, bool(finish), together, s...  88.9 us
    ppermute x10, waiting for transfers between devices, shards(): lax.ppermute(part, axis, [(i, turn(i, stride, size, shift)) for i in rang...  80 us
    pallas_call x1, Pallas kernels, shards(): pl.pallas_call(local_kernel, name='local', out_shape=[shapes((nblocks, D,...  60.7 us
    all_to_all x3, waiting for transfers between devices, shards(): lax.all_to_all(slots, AXES, split_axis=0, concat_axis=0, tiled=True)  44.6 us
    all_to_all x3, starting transfers between devices, shards(): lax.all_to_all(slots, AXES, split_axis=0, concat_axis=0, tiled=True)  28.7 us
    ppermute x10, starting transfers between devices, shards(): lax.ppermute(part, axis, [(i, turn(i, stride, size, shift)) for i in rang...  15.5 us
    ppermute x4, starting transfers between devices, shift(): return lax.ppermute(edge, axis, pairs)  13.5 us
    pallas_call x3, Pallas kernels, shards(): pl.pallas_call(functools.partial(send_kernel, first, (blocks_x, blocks_y)...  11.8 us
  transfers between devices with their start and end apart: 17, of which 6 were waited for; matrix products, arithmetic and copies ran while one was open for 3% of the time, Pallas kernels for 40%

profile of v3, /device:TPU:14, one launch (start us, length us, event | category | flops | bytes accessed | tf_op | source)
XLA Modules:
  0.0 358.0 jit_solution(8800501162546398414)
XLA Ops:
  0.6 4.1 %shard_map.105 = (bf16[128,32,512]{2,1,0:T(8,128)(2,1)}, bf16[4,128,512]{2,1,0:T(8,128)(2,1)}, bf16[4,128,512]{2,1,0:T(8,128)(2,1)}, bf16[4,128,512]{2,1,0:T(8,128)(2,1)}, bf16[4,128,512]{2,1,0:T(8,128)(2,1)}) custom-call(s32[4,4,4]{2,1,0:T(4,128)} %table.5, bf16[16,128,512]{2,1,0:T(8,128)(2,1)} %bitcast.14), custom_call_target="tpu_custom_call" | custom-call | bytes 10485760 | tf_op jit(solution)/shard_map/pallas_call | solution.py:318
  4.7 10.8 %all-to-all-start.1 = ((bf16[128,32,512]{2,1,0:T(8,128)(2,1)}), bf16[128,32,512]{2,1,0:T(8,128)(2,1)}, u32[]{:S(2)}, u32[]{:S(2)}) async-start(bf16[128,32,512]{2,1,0:T(8,128)(2,1)} %get-tuple-element.22), calls=%async_computation.1 | async-start | bytes 8388608 | tf_op jit(solution)/shard_map/all_to_all | solution.py:336
  15.6 4.1 %shard_map.106 = bf16[128,64,512]{2,1,0:T(8,128)(2,1)} custom-call(s32[4,4,4]{2,1,0:T(4,128)} %table.5, bf16[16,128,512]{2,1,0:T(8,128)(2,1)} %bitcast.15), custom_call_target="tpu_custom_call" | custom-call | bytes 10485760 | tf_op jit(solution)/shard_map/pallas_call | solution.py:318
  21.8 44.6 %all-to-all-done.1.refs_0_.refs_1_.refs_2_.refs_3_.refs_4_.refs_5_.refs_6_.refs_7_.refs_8_.refs_9_.refs_10_.refs_11_.refs_12_.refs_13_.refs_14_.refs_15_ = bf16[128,32,512]{2,1,0:T(8,128)(2,1)} async-done(((bf16[128,32,512]{2,1,0:T(8,128)(2,1)}), bf16[128,32,512]{2,1,0:T(8,128)(2,1)}, u32[]{:S(2)}, u32[]{:S(2)}) %all-to-all-start.1) | async-done | bytes 4194336 | tf_op jit(solution)/shard_map/all_to_all | solution.py:336
  66.4 7.5 %all-to-all-start.2 = ((bf16[128,64,512]{2,1,0:T(8,128)(2,1)}), bf16[128,64,512]{2,1,0:T(8,128)(2,1)}, u32[]{:S(2)}, u32[]{:S(2)}) async-start(bf16[128,64,512]{2,1,0:T(8,128)(2,1)} %shard_map.106), calls=%async_computation.2 | async-start | bytes 16777216 | tf_op jit(solution)/shard_map/all_to_all | solution.py:336
  77.7 60.7 %local.1 = (bf16[16,512,128]{2,1,0:T(8,128)(2,1)}, f32[16,512,128]{2,1,0:T(8,128)}, f32[16,8,128]{2,1,0:T(8,128)}, f32[16,8,128]{2,1,0:T(8,128)}, f32[12,512]{1,0:T(8,128)}) custom-call(s32[4,4,4]{2,1,0:T(4,128)} %and_convert_fusion.live, bf16[16,128,512]{2,1,0:T(8,128)(2,1)} %bitcast.16, bf16[16,128,512]{2,1,0:T(8,128)(2,1)} %bitcast.17, ...), custom_call_target="tpu_custom_call" | custom-call | flops 40000000000 | bytes 31457280 | tf_op jit(solution)/shard_map/local/pallas_call | solution.py:398
  142.8 2.1 collective-permute-start.7
  144.9 29.1 %collective-permute-done.5 = f32[12,512]{1,0:T(8,128)S(1)} collective-permute-done((f32[12,512]{1,0:T(8,128)S(1)}, f32[12,512]{1,0:T(8,128)S(1)}, u32[]{:S(2)}, u32[]{:S(2)}) %collective-permute-start.5) | collective-permute-done | bytes 24608 | tf_op jit(solution)/shard_map/ppermute | solution.py:499
  174.6 2.0 collective-permute-start.8
  176.6 1.8 collective-permute-start.9
  178.4 2.9 collective-permute-start
  181.3 5.0 %collective-permute-start.1 = (bf16[4,128,512]{2,1,0:T(8,128)(2,1)}, bf16[4,128,512]{2,1,0:T(8,128)(2,1)S(1)}, u32[]{:S(2)}, u32[]{:S(2)}) collective-permute-start(bf16[4,128,512]{2,1,0:T(8,128)(2,1)} %get-tuple-element.24), channel_id=1, source_target_pairs={{8,0},{16,8},{24,16},{32,24},{40,32},{48,40},{56,48},{64,56},{72,6... | collective-permute-start | bytes 1572872 | tf_op jit(solution)/shard_map/ppermute | solution.py:291
  186.5 3.6 shard_map.104
  190.0 1.9 collective-permute-start.2
  192.0 3.6 %collective-permute-start.3 = (bf16[4,128,512]{2,1,0:T(8,128)(2,1)S(1)}, bf16[4,128,512]{2,1,0:T(8,128)(2,1)S(1)}, u32[]{:S(2)}, u32[]{:S(2)}) collective-permute-start(bf16[4,128,512]{2,1,0:T(8,128)(2,1)S(1)} %copy-done.9), channel_id=1, source_target_pairs={{1,0},{2,1},{3,2},{4,3},{5,4},{6,5},{7,6},{9,8},{10,9},{11,10},{12... | collective-permute-start | bytes 1572872 | tf_op jit(solution)/shard_map/ppermute | solution.py:291
  195.7 10.3 %all-to-all-start = ((bf16[128,32,512]{2,1,0:T(8,128)(2,1)}), bf16[128,32,512]{2,1,0:T(8,128)(2,1)}, u32[]{:S(2)}, u32[]{:S(2)}) async-start(bf16[128,32,512]{2,1,0:T(8,128)(2,1)} %shard_map.104), calls=%async_computation | async-start | bytes 8388608 | tf_op jit(solution)/shard_map/all_to_all | solution.py:336
  208.1 42.9 %collective-permute-done.11.refs_1_ = f32[12,512]{1,0:T(8,128)S(1)} collective-permute-done((f32[12,512]{1,0:T(8,128)S(1)}, f32[12,512]{1,0:T(8,128)S(1)}, u32[]{:S(2)}, u32[]{:S(2)}) %collective-permute-start.11) | collective-permute-done | bytes 24608 | tf_op jit(solution)/shard_map/ppermute | solution.py:499
  251.2 6.3 %collective-permute-done.12.refs_2_ = f32[12,512]{1,0:T(8,128)S(1)} collective-permute-done((f32[12,512]{1,0:T(8,128)S(1)}, f32[12,512]{1,0:T(8,128)S(1)}, u32[]{:S(2)}, u32[]{:S(2)}) %collective-permute-start.12) | collective-permute-done | bytes 24608 | tf_op jit(solution)/shard_map/ppermute | solution.py:499
  257.5 5.5 %collective-permute-start.13 = (f32[12,512]{1,0:T(8,128)S(1)}, f32[12,512]{1,0:T(8,128)S(1)}, u32[]{:S(2)}, u32[]{:S(2)}) collective-permute-start(f32[12,512]{1,0:T(8,128)S(1)} %pad_maximum_fusion.3.refs_0_), channel_id=1, source_target_pairs={{0,24},{8,0},{16,8},{24,16},{32,56},{40,32},{48,40},{56,48},{64,88... | collective-permute-start | bytes 73736 | tf_op jit(solution)/shard_map/ppermute | solution.py:499
  265.4 2.0 finish.1
  269.0 31.7 %shard_map.107 = (f32[16,512,128]{2,1,0:T(8,128)}, f32[16,8,128]{2,1,0:T(8,128)}, f32[16,8,128]{2,1,0:T(8,128)}) custom-call(s32[4,4,4]{2,1,0:T(4,128)} %table.5, bf16[128,64,512]{2,1,0:T(8,128)(2,1)} %all-to-all-done.2.refs_0_.refs_1_.refs_2_.refs_3_.refs_4_.refs_5_.refs_6_.refs_7_, ...), custom_call_target="tpu_custom_call" | custom-call | flops 12800000000 | bytes 20971520 | tf_op jit(solution)/shard_map/pallas_call | solution.py:452
  300.6 28.3 %shard_map.108 = (f32[16,512,128]{2,1,0:T(8,128)}, f32[16,8,128]{2,1,0:T(8,128)}, f32[16,8,128]{2,1,0:T(8,128)}) custom-call(s32[32]{0:T(128)} %reshape.132.table, bf16[16,128,512]{2,1,0:T(8,128)(2,1)} %pad_maximum_fusion.refs_0_.refs_1_.refs_2_.refs_3_, bf16[16,128,512]{2,1,0:T(8,128)(2,1)} %pad_maximum_fusion.refs_0_.refs_1_.refs_2_.refs_3_, ...), custom_call_target="tpu_custom_call" | custom-call | flops 12800000000 | bytes 20971520 | tf_op jit(solution)/shard_map/pallas_call | solution.py:452
  328.9 13.8 %shard_map.109 = (f32[16,512,128]{2,1,0:T(8,128)}, f32[16,8,128]{2,1,0:T(8,128)}, f32[16,8,128]{2,1,0:T(8,128)}) custom-call(s32[4,4,4]{2,1,0:T(4,128)} %table.5, bf16[128,32,512]{2,1,0:T(8,128)(2,1)} %all-to-all-done.1.refs_0_.refs_1_.refs_2_.refs_3_.refs_4_.refs_5_.refs_6_.refs_7_.refs_8_.refs_9_.refs_10_.refs_11_.refs_12_.refs_13_.refs_14_.refs_15_, ...), custom_call_target="tpu_custom_call" | custom-call | flops 6400000000 | bytes 20971520 | tf_op jit(solution)/shard_map/pallas_call | solution.py:452
  342.8 15.1 %shard_map.110 = bf16[16,128,512]{2,1,0:T(8,128)(2,1)} custom-call(s32[4,4,4]{2,1,0:T(4,128)} %table.5, bf16[128,32,512]{2,1,0:T(8,128)(2,1)} %all-to-all-done.refs_0_.refs_1_.refs_2_.refs_3_.refs_4_.refs_5_.refs_6_.refs_7_.refs_8_.refs_9_.refs_10_.refs_11_.refs_12_.refs_13_.refs_14_.refs_15_, ...), custom_call_target="tpu_custom_call" | custom-call | flops 6400000000 | bytes 20971520 | tf_op jit(solution)/shard_map/pallas_call | solution.py:452
  (95 shorter events, 16.9 us)
Async XLA Ops:
  4.7 61.6 %all-to-all-start.1 = ((bf16[128,32,512]{2,1,0:T(8,128)(2,1)}), bf16[128,32,512]{2,1,0:T(8,128)(2,1)}, u32[]{:S(2)}, u32[]{:S(2)}) async-start(bf16[128,32,512]{2,1,0:T(8,128)(2,1)} %get-tuple-element.22), calls=%async_computation.1 | async-start | bytes 8388608 | tf_op jit(solution)/shard_map/all_to_all | solution.py:336
  15.6 5.2 %copy-start.1 = (bf16[512,512]{1,0:T(8,128)(2,1)S(1)}, bf16[512,512]{1,0:T(8,128)(2,1)}, u32[]{:S(2)}) copy-start(bf16[512,512]{1,0:T(8,128)(2,1)} %param.11) | copy-start | bytes 1572868
  21.8 52.1 %copy-start = (bf16[512,512]{1,0:T(8,128)(2,1)S(1)}, bf16[512,512]{1,0:T(8,128)(2,1)}, u32[]{:S(2)}) copy-start(bf16[512,512]{1,0:T(8,128)(2,1)} %refs_20_.3) | copy-start | bytes 1572868
  21.8 52.1 %copy-start.8 = (bf16[4,512]{1,0:T(4,128)(2,1)S(1)}, bf16[4,512]{1,0:T(4,128)(2,1)}, u32[]{:S(2)}) copy-start(bf16[4,512]{1,0:T(4,128)(2,1)} %refs_5_.1) | copy-start | bytes 12292
  66.4 129.4 %all-to-all-start.2 = ((bf16[128,64,512]{2,1,0:T(8,128)(2,1)}), bf16[128,64,512]{2,1,0:T(8,128)(2,1)}, u32[]{:S(2)}, u32[]{:S(2)}) async-start(bf16[128,64,512]{2,1,0:T(8,128)(2,1)} %shard_map.106), calls=%async_computation.2 | async-start | bytes 16777216 | tf_op jit(solution)/shard_map/all_to_all | solution.py:336
  138.5 1.5 collective-permute-start.4
  140.8 33.2 %collective-permute-start.5 = (f32[12,512]{1,0:T(8,128)S(1)}, f32[12,512]{1,0:T(8,128)S(1)}, u32[]{:S(2)}, u32[]{:S(2)}) collective-permute-start(f32[12,512]{1,0:T(8,128)S(1)} %pad_maximum_fusion.1), channel_id=1, source_target_pairs={{0,6},{1,7},{2,0},{3,1},{4,2},{5,3},{6,4},{7,5},{8,14},{9,15},{10,... | collective-permute-start | bytes 73736 | tf_op jit(solution)/shard_map/ppermute | solution.py:499
  141.7 32.7 %collective-permute-start.6 = (f32[12,512]{1,0:T(8,128)S(1)}, f32[12,512]{1,0:T(8,128)S(1)}, u32[]{:S(2)}, u32[]{:S(2)}) collective-permute-start(f32[12,512]{1,0:T(8,128)S(1)} %pad_maximum_fusion.1), channel_id=1, source_target_pairs={{0,4},{1,5},{2,6},{3,7},{4,0},{5,1},{6,2},{7,3},{8,12},{9,13},{10,... | collective-permute-start | bytes 73736 | tf_op jit(solution)/shard_map/ppermute | solution.py:499
  142.8 31.5 %collective-permute-start.7 = (f32[12,512]{1,0:T(8,128)S(1)}, f32[12,512]{1,0:T(8,128)S(1)}, u32[]{:S(2)}, u32[]{:S(2)}) collective-permute-start(f32[12,512]{1,0:T(8,128)S(1)} %pad_maximum_fusion.1), channel_id=1, source_target_pairs={{0,2},{1,3},{2,4},{3,5},{4,6},{5,7},{6,0},{7,1},{8,10},{9,11},{10,... | collective-permute-start | bytes 73736 | tf_op jit(solution)/shard_map/ppermute | solution.py:499
  174.5 15.5 %collective-permute-start.10 = (f32[12,512]{1,0:T(8,128)S(1)}, f32[12,512]{1,0:T(8,128)S(1)}, u32[]{:S(2)}, u32[]{:S(2)}) collective-permute-start(f32[12,512]{1,0:T(8,128)S(1)} %pad_maximum_fusion.2), channel_id=1, source_target_pairs={{0,32},{8,40},{16,48},{24,56},{32,64},{40,72},{48,80},{56,88},{64,... | collective-permute-start | bytes 73736 | tf_op jit(solution)/shard_map/ppermute | solution.py:499
  174.6 17.4 %collective-permute-start.8 = (f32[12,512]{1,0:T(8,128)S(1)}, f32[12,512]{1,0:T(8,128)S(1)}, u32[]{:S(2)}, u32[]{:S(2)}) collective-permute-start(f32[12,512]{1,0:T(8,128)S(1)} %pad_maximum_fusion.2), channel_id=1, source_target_pairs={{0,96},{8,104},{16,112},{24,120},{32,0},{40,8},{48,16},{56,24},{64... | collective-permute-start | bytes 73736 | tf_op jit(solution)/shard_map/ppermute | solution.py:499
  176.6 19.1 %collective-permute-start.9 = (f32[12,512]{1,0:T(8,128)S(1)}, f32[12,512]{1,0:T(8,128)S(1)}, u32[]{:S(2)}, u32[]{:S(2)}) collective-permute-start(f32[12,512]{1,0:T(8,128)S(1)} %pad_maximum_fusion.2), channel_id=1, source_target_pairs={{0,64},{8,72},{16,80},{24,88},{32,96},{40,104},{48,112},{56,120},{... | collective-permute-start | bytes 73736 | tf_op jit(solution)/shard_map/ppermute | solution.py:499
  178.4 89.0 %collective-permute-start = (bf16[4,128,512]{2,1,0:T(8,128)(2,1)}, bf16[4,128,512]{2,1,0:T(8,128)(2,1)S(1)}, u32[]{:S(2)}, u32[]{:S(2)}) collective-permute-start(bf16[4,128,512]{2,1,0:T(8,128)(2,1)} %get-tuple-element.23), channel_id=1, source_target_pairs={{0,8},{8,16},{16,24},{24,32},{32,40},{40,48},{48,56},{56,64},{64,7... | collective-permute-start | bytes 1572872 | tf_op jit(solution)/shard_map/ppermute | solution.py:291
  181.3 86.1 %collective-permute-start.1 = (bf16[4,128,512]{2,1,0:T(8,128)(2,1)}, bf16[4,128,512]{2,1,0:T(8,128)(2,1)S(1)}, u32[]{:S(2)}, u32[]{:S(2)}) collective-permute-start(bf16[4,128,512]{2,1,0:T(8,128)(2,1)} %get-tuple-element.24), channel_id=1, source_target_pairs={{8,0},{16,8},{24,16},{32,24},{40,32},{48,40},{56,48},{64,56},{72,6... | collective-permute-start | bytes 1572872 | tf_op jit(solution)/shard_map/ppermute | solution.py:291
  186.4 5.5 %copy-start.9 = (bf16[4,128,512]{2,1,0:T(8,128)(2,1)S(1)}, bf16[4,128,512]{2,1,0:T(8,128)(2,1)}, u32[]{:S(2)}) copy-start(bf16[4,128,512]{2,1,0:T(8,128)(2,1)} %get-tuple-element.26) | copy-start | bytes 1572868
  190.0 77.3 %collective-permute-start.2 = (bf16[4,128,512]{2,1,0:T(8,128)(2,1)S(1)}, bf16[4,128,512]{2,1,0:T(8,128)(2,1)S(1)}, u32[]{:S(2)}, u32[]{:S(2)}) collective-permute-start(bf16[4,128,512]{2,1,0:T(8,128)(2,1)S(1)} %copy-done.10), channel_id=1, source_target_pairs={{0,1},{1,2},{2,3},{3,4},{4,5},{5,6},{6,7},{8,9},{9,10},{10,11},{11... | collective-permute-start | bytes 1572872 | tf_op jit(solution)/shard_map/ppermute | solution.py:291
  192.0 75.4 %collective-permute-start.3 = (bf16[4,128,512]{2,1,0:T(8,128)(2,1)S(1)}, bf16[4,128,512]{2,1,0:T(8,128)(2,1)S(1)}, u32[]{:S(2)}, u32[]{:S(2)}) collective-permute-start(bf16[4,128,512]{2,1,0:T(8,128)(2,1)S(1)} %copy-done.9), channel_id=1, source_target_pairs={{1,0},{2,1},{3,2},{4,3},{5,4},{6,5},{7,6},{9,8},{10,9},{11,10},{12... | collective-permute-start | bytes 1572872 | tf_op jit(solution)/shard_map/ppermute | solution.py:291
  195.7 147.0 %all-to-all-start = ((bf16[128,32,512]{2,1,0:T(8,128)(2,1)}), bf16[128,32,512]{2,1,0:T(8,128)(2,1)}, u32[]{:S(2)}, u32[]{:S(2)}) async-start(bf16[128,32,512]{2,1,0:T(8,128)(2,1)} %shard_map.104), calls=%async_computation | async-start | bytes 8388608 | tf_op jit(solution)/shard_map/all_to_all | solution.py:336
  206.1 58.6 %copy-start.3 = (f32[12,512]{1,0:T(8,128)}, f32[12,512]{1,0:T(8,128)S(1)}, u32[]{:S(2)}) copy-start(f32[12,512]{1,0:T(8,128)S(1)} %pad_maximum_fusion.3.refs_0_) | copy-start | bytes 73732
  206.1 44.8 %collective-permute-start.11 = (f32[12,512]{1,0:T(8,128)S(1)}, f32[12,512]{1,0:T(8,128)S(1)}, u32[]{:S(2)}, u32[]{:S(2)}) collective-permute-start(f32[12,512]{1,0:T(8,128)S(1)} %pad_maximum_fusion.3.refs_0_), channel_id=1, source_target_pairs={{0,8},{8,16},{16,24},{24,0},{32,40},{40,48},{48,56},{56,32},{64,72... | collective-permute-start | bytes 73736 | tf_op jit(solution)/shard_map/ppermute | solution.py:499
  251.0 13.8 %copy-start.4 = (f32[12,512]{1,0:T(8,128)}, f32[12,512]{1,0:T(8,128)S(1)}, u32[]{:S(2)}) copy-start(f32[12,512]{1,0:T(8,128)S(1)} %collective-permute-done.11.refs_1_) | copy-start | bytes 73732
  251.0 6.5 %collective-permute-start.12 = (f32[12,512]{1,0:T(8,128)S(1)}, f32[12,512]{1,0:T(8,128)S(1)}, u32[]{:S(2)}, u32[]{:S(2)}) collective-permute-start(f32[12,512]{1,0:T(8,128)S(1)} %pad_maximum_fusion.3.refs_0_), channel_id=1, source_target_pairs={{0,16},{8,24},{16,0},{24,8},{32,48},{40,56},{48,32},{56,40},{64,80... | collective-permute-start | bytes 73736 | tf_op jit(solution)/shard_map/ppermute | solution.py:499
  257.5 7.2 %copy-start.5 = (f32[12,512]{1,0:T(8,128)}, f32[12,512]{1,0:T(8,128)S(1)}, u32[]{:S(2)}) copy-start(f32[12,512]{1,0:T(8,128)S(1)} %collective-permute-done.12.refs_2_) | copy-start | bytes 73732
  257.5 7.2 %collective-permute-start.13 = (f32[12,512]{1,0:T(8,128)S(1)}, f32[12,512]{1,0:T(8,128)S(1)}, u32[]{:S(2)}, u32[]{:S(2)}) collective-permute-start(f32[12,512]{1,0:T(8,128)S(1)} %pad_maximum_fusion.3.refs_0_), channel_id=1, source_target_pairs={{0,24},{8,0},{16,8},{24,16},{32,56},{40,32},{48,40},{56,48},{64,88... | collective-permute-start | bytes 73736 | tf_op jit(solution)/shard_map/ppermute | solution.py:499
  (4 other events, 10.8 us)

commit v4 on v3

--- a/solution.py
+++ b/solution.py
@@ -34,7 +34,8 @@
 
 def device_of(partner, blocks_x, blocks_y, mesh_cols):
     grid_cols = blocks_y * mesh_cols
-    return partner // grid_cols // blocks_x * mesh_cols + partner % grid_cols // blocks_y
+    row, col = lax.div(partner, grid_cols * blocks_x), lax.div(lax.rem(partner, grid_cols), blocks_y)
+    return row * mesh_cols + col
 
 
 def send_kernel(first, sides, where_to, partners, feats, *refs):
@@ -476,7 +477,7 @@
 
     state = add_keys(arrived[0], SPLIT[0], TOGETHER[0], NEXP, partners, partner_block, state)
     edge_blocks = jnp.concatenate(edges_in, axis=0)
-    state = add_keys(edge_blocks, BLK, TOGETHER[0], 2, far_live, edge_block, state)
+    state = add_keys(edge_blocks, BLK, 4, 2, far_live, edge_block, state)
     state = add_keys(arrived[1], SPLIT[1], TOGETHER[1], NEXP, partners, partner_block, state)
     node_out = add_keys(
         arrived[2], SPLIT[2], TOGETHER[2], NEXP, partners, partner_block, state,

time: 359 us -> 354 us (0.986)
  Pallas kernels: 163 us -> 158 us
    pallas_call x4, Pallas kernels: 88.9 us -> 83.5 us  [add_keys(): pl.pallas_call(functools.partial(remote_kernel, bool(finish), together, s...]
where the time goes in v4:
time: 354 us; the launch traced here: 353 us
  Pallas kernels  158 us (45%)
  waiting for transfers between devices  125 us (35%)
  starting transfers between devices  57.6 us (16%)
  local copies, waits for them, and re-layouts  5.95 us (2%)
  other arithmetic  4.89 us (1%)
    pallas_call x4, Pallas kernels, add_keys(): pl.pallas_call(functools.partial(remote_kernel, bool(finish), together, s...  83.5 us
    ppermute x10, waiting for transfers between devices, shards(): lax.ppermute(part, axis, [(i, turn(i, stride, size, shift)) for i in rang...  80 us
    pallas_call x1, Pallas kernels, shards(): pl.pallas_call(local_kernel, name='local', out_shape=[shapes((nblocks, D,...  60.7 us
    all_to_all x3, waiting for transfers between devices, shards(): lax.all_to_all(slots, AXES, split_axis=0, concat_axis=0, tiled=True)  44.6 us
    all_to_all x3, starting transfers between devices, shards(): lax.all_to_all(slots, AXES, split_axis=0, concat_axis=0, tiled=True)  28.7 us
    ppermute x10, starting transfers between devices, shards(): lax.ppermute(part, axis, [(i, turn(i, stride, size, shift)) for i in rang...  15.5 us
    ppermute x4, starting transfers between devices, shift(): return lax.ppermute(edge, axis, pairs)  13.5 us
    pallas_call x3, Pallas kernels, shards(): pl.pallas_call(functools.partial(send_kernel, first, (blocks_x, blocks_y)...  11.7 us
  transfers between devices with their start and end apart: 17, of which 6 were waited for; matrix products, arithmetic and copies ran while one was open for 3% of the time, Pallas kernels for 40%

profile of v4, /device:TPU:14, one launch (start us, length us, event | category | flops | bytes accessed | tf_op | source)
XLA Modules:
  0.0 352.5 jit_solution(13060006566699513715)
XLA Ops:
  0.6 4.0 %shard_map.105 = (bf16[128,32,512]{2,1,0:T(8,128)(2,1)}, bf16[4,128,512]{2,1,0:T(8,128)(2,1)}, bf16[4,128,512]{2,1,0:T(8,128)(2,1)}, bf16[4,128,512]{2,1,0:T(8,128)(2,1)}, bf16[4,128,512]{2,1,0:T(8,128)(2,1)}) custom-call(s32[4,4,4]{2,1,0:T(4,128)} %table.5, bf16[16,128,512]{2,1,0:T(8,128)(2,1)} %bitcast.14), custom_call_target="tpu_custom_call" | custom-call | bytes 10485760 | tf_op jit(solution)/shard_map/pallas_call | solution.py:319
  4.6 10.9 %all-to-all-start.1 = ((bf16[128,32,512]{2,1,0:T(8,128)(2,1)}), bf16[128,32,512]{2,1,0:T(8,128)(2,1)}, u32[]{:S(2)}, u32[]{:S(2)}) async-start(bf16[128,32,512]{2,1,0:T(8,128)(2,1)} %get-tuple-element.22), calls=%async_computation.1 | async-start | bytes 8388608 | tf_op jit(solution)/shard_map/all_to_all | solution.py:337
  15.6 4.1 %shard_map.106 = bf16[128,64,512]{2,1,0:T(8,128)(2,1)} custom-call(s32[4,4,4]{2,1,0:T(4,128)} %table.5, bf16[16,128,512]{2,1,0:T(8,128)(2,1)} %bitcast.15), custom_call_target="tpu_custom_call" | custom-call | bytes 10485760 | tf_op jit(solution)/shard_map/pallas_call | solution.py:319
  21.7 44.6 %all-to-all-done.1.refs_0_.refs_1_.refs_2_.refs_3_.refs_4_.refs_5_.refs_6_.refs_7_.refs_8_.refs_9_.refs_10_.refs_11_.refs_12_.refs_13_.refs_14_.refs_15_ = bf16[128,32,512]{2,1,0:T(8,128)(2,1)} async-done(((bf16[128,32,512]{2,1,0:T(8,128)(2,1)}), bf16[128,32,512]{2,1,0:T(8,128)(2,1)}, u32[]{:S(2)}, u32[]{:S(2)}) %all-to-all-start.1) | async-done | bytes 4194336 | tf_op jit(solution)/shard_map/all_to_all | solution.py:337
  66.3 7.5 %all-to-all-start.2 = ((bf16[128,64,512]{2,1,0:T(8,128)(2,1)}), bf16[128,64,512]{2,1,0:T(8,128)(2,1)}, u32[]{:S(2)}, u32[]{:S(2)}) async-start(bf16[128,64,512]{2,1,0:T(8,128)(2,1)} %shard_map.106), calls=%async_computation.2 | async-start | bytes 16777216 | tf_op jit(solution)/shard_map/all_to_all | solution.py:337
  77.7 60.7 %local.1 = (bf16[16,512,128]{2,1,0:T(8,128)(2,1)}, f32[16,512,128]{2,1,0:T(8,128)}, f32[16,8,128]{2,1,0:T(8,128)}, f32[16,8,128]{2,1,0:T(8,128)}, f32[12,512]{1,0:T(8,128)}) custom-call(s32[4,4,4]{2,1,0:T(4,128)} %and_convert_fusion.live, bf16[16,128,512]{2,1,0:T(8,128)(2,1)} %bitcast.16, bf16[16,128,512]{2,1,0:T(8,128)(2,1)} %bitcast.17, ...), custom_call_target="tpu_custom_call" | custom-call | flops 40000000000 | bytes 31457280 | tf_op jit(solution)/shard_map/local/pallas_call | solution.py:399
  142.8 2.1 collective-permute-start.7
  144.9 29.1 %collective-permute-done.5 = f32[12,512]{1,0:T(8,128)S(1)} collective-permute-done((f32[12,512]{1,0:T(8,128)S(1)}, f32[12,512]{1,0:T(8,128)S(1)}, u32[]{:S(2)}, u32[]{:S(2)}) %collective-permute-start.5) | collective-permute-done | bytes 24608 | tf_op jit(solution)/shard_map/ppermute | solution.py:500
  174.5 2.0 collective-permute-start.8
  176.5 1.8 collective-permute-start.9
  178.3 2.9 collective-permute-start
  181.3 5.0 %collective-permute-start.1 = (bf16[4,128,512]{2,1,0:T(8,128)(2,1)}, bf16[4,128,512]{2,1,0:T(8,128)(2,1)S(1)}, u32[]{:S(2)}, u32[]{:S(2)}) collective-permute-start(bf16[4,128,512]{2,1,0:T(8,128)(2,1)} %get-tuple-element.24), channel_id=1, source_target_pairs={{8,0},{16,8},{24,16},{32,24},{40,32},{48,40},{56,48},{64,56},{72,6... | collective-permute-start | bytes 1572872 | tf_op jit(solution)/shard_map/ppermute | solution.py:292
  186.4 3.5 %shard_map.104 = bf16[128,32,512]{2,1,0:T(8,128)(2,1)} custom-call(s32[4,4,4]{2,1,0:T(4,128)} %table.5, bf16[16,128,512]{2,1,0:T(8,128)(2,1)} %bitcast.21), custom_call_target="tpu_custom_call" | custom-call | bytes 10485760 | tf_op jit(solution)/shard_map/pallas_call | solution.py:319
  190.0 1.9 collective-permute-start.2
  191.9 3.6 %collective-permute-start.3 = (bf16[4,128,512]{2,1,0:T(8,128)(2,1)S(1)}, bf16[4,128,512]{2,1,0:T(8,128)(2,1)S(1)}, u32[]{:S(2)}, u32[]{:S(2)}) collective-permute-start(bf16[4,128,512]{2,1,0:T(8,128)(2,1)S(1)} %copy-done.9), channel_id=1, source_target_pairs={{1,0},{2,1},{3,2},{4,3},{5,4},{6,5},{7,6},{9,8},{10,9},{11,10},{12... | collective-permute-start | bytes 1572872 | tf_op jit(solution)/shard_map/ppermute | solution.py:292
  195.7 10.3 %all-to-all-start = ((bf16[128,32,512]{2,1,0:T(8,128)(2,1)}), bf16[128,32,512]{2,1,0:T(8,128)(2,1)}, u32[]{:S(2)}, u32[]{:S(2)}) async-start(bf16[128,32,512]{2,1,0:T(8,128)(2,1)} %shard_map.104), calls=%async_computation | async-start | bytes 8388608 | tf_op jit(solution)/shard_map/all_to_all | solution.py:337
  208.0 42.9 %collective-permute-done.11.refs_1_ = f32[12,512]{1,0:T(8,128)S(1)} collective-permute-done((f32[12,512]{1,0:T(8,128)S(1)}, f32[12,512]{1,0:T(8,128)S(1)}, u32[]{:S(2)}, u32[]{:S(2)}) %collective-permute-start.11) | collective-permute-done | bytes 24608 | tf_op jit(solution)/shard_map/ppermute | solution.py:500
  251.1 6.3 %collective-permute-done.12.refs_2_ = f32[12,512]{1,0:T(8,128)S(1)} collective-permute-done((f32[12,512]{1,0:T(8,128)S(1)}, f32[12,512]{1,0:T(8,128)S(1)}, u32[]{:S(2)}, u32[]{:S(2)}) %collective-permute-start.12) | collective-permute-done | bytes 24608 | tf_op jit(solution)/shard_map/ppermute | solution.py:500
  257.4 5.5 %collective-permute-start.13 = (f32[12,512]{1,0:T(8,128)S(1)}, f32[12,512]{1,0:T(8,128)S(1)}, u32[]{:S(2)}, u32[]{:S(2)}) collective-permute-start(f32[12,512]{1,0:T(8,128)S(1)} %pad_maximum_fusion.3.refs_0_), channel_id=1, source_target_pairs={{0,24},{8,0},{16,8},{24,16},{32,56},{40,32},{48,40},{56,48},{64,88... | collective-permute-start | bytes 73736 | tf_op jit(solution)/shard_map/ppermute | solution.py:500
  265.3 2.0 finish.1
  268.9 29.8 %shard_map.107 = (f32[16,512,128]{2,1,0:T(8,128)}, f32[16,8,128]{2,1,0:T(8,128)}, f32[16,8,128]{2,1,0:T(8,128)}) custom-call(s32[4,4,4]{2,1,0:T(4,128)} %table.5, bf16[128,64,512]{2,1,0:T(8,128)(2,1)} %all-to-all-done.2.refs_0_.refs_1_.refs_2_.refs_3_.refs_4_.refs_5_.refs_6_.refs_7_, ...), custom_call_target="tpu_custom_call" | custom-call | flops 12800000000 | bytes 20971520 | tf_op jit(solution)/shard_map/pallas_call | solution.py:453
  298.7 28.3 %shard_map.108 = (f32[16,512,128]{2,1,0:T(8,128)}, f32[16,8,128]{2,1,0:T(8,128)}, f32[16,8,128]{2,1,0:T(8,128)}) custom-call(s32[32]{0:T(128)} %reshape.132.table, bf16[16,128,512]{2,1,0:T(8,128)(2,1)} %pad_maximum_fusion.refs_0_.refs_1_.refs_2_.refs_3_.refs_4_.refs_5_.refs_6_.refs_7_, ...), custom_call_target="tpu_custom_call" | custom-call | flops 12800000000 | bytes 20971520 | tf_op jit(solution)/shard_map/pallas_call | solution.py:453
  327.0 12.0 %shard_map.109 = (f32[16,512,128]{2,1,0:T(8,128)}, f32[16,8,128]{2,1,0:T(8,128)}, f32[16,8,128]{2,1,0:T(8,128)}) custom-call(s32[4,4,4]{2,1,0:T(4,128)} %table.5, bf16[128,32,512]{2,1,0:T(8,128)(2,1)} %all-to-all-done.1.refs_0_.refs_1_.refs_2_.refs_3_.refs_4_.refs_5_.refs_6_.refs_7_.refs_8_.refs_9_.refs_10_.refs_11_.refs_12_.refs_13_.refs_14_.refs_15_, ...), custom_call_target="tpu_custom_call" | custom-call | flops 6400000000 | bytes 20971520 | tf_op jit(solution)/shard_map/pallas_call | solution.py:453
  339.0 13.4 %shard_map.110 = bf16[16,128,512]{2,1,0:T(8,128)(2,1)} custom-call(s32[4,4,4]{2,1,0:T(4,128)} %table.5, bf16[128,32,512]{2,1,0:T(8,128)(2,1)} %all-to-all-done.refs_0_.refs_1_.refs_2_.refs_3_.refs_4_.refs_5_.refs_6_.refs_7_.refs_8_.refs_9_.refs_10_.refs_11_.refs_12_.refs_13_.refs_14_.refs_15_, ...), custom_call_target="tpu_custom_call" | custom-call | flops 6400000000 | bytes 20971520 | tf_op jit(solution)/shard_map/pallas_call | solution.py:453
  (95 shorter events, 16.9 us)
Async XLA Ops:
  4.6 61.7 %all-to-all-start.1 = ((bf16[128,32,512]{2,1,0:T(8,128)(2,1)}), bf16[128,32,512]{2,1,0:T(8,128)(2,1)}, u32[]{:S(2)}, u32[]{:S(2)}) async-start(bf16[128,32,512]{2,1,0:T(8,128)(2,1)} %get-tuple-element.22), calls=%async_computation.1 | async-start | bytes 8388608 | tf_op jit(solution)/shard_map/all_to_all | solution.py:337
  15.6 5.2 %copy-start.1 = (bf16[512,512]{1,0:T(8,128)(2,1)S(1)}, bf16[512,512]{1,0:T(8,128)(2,1)}, u32[]{:S(2)}) copy-start(bf16[512,512]{1,0:T(8,128)(2,1)} %param.11) | copy-start | bytes 1572868
  21.7 52.1 %copy-start = (bf16[512,512]{1,0:T(8,128)(2,1)S(1)}, bf16[512,512]{1,0:T(8,128)(2,1)}, u32[]{:S(2)}) copy-start(bf16[512,512]{1,0:T(8,128)(2,1)} %refs_20_.3) | copy-start | bytes 1572868
  21.7 52.1 %copy-start.8 = (bf16[4,512]{1,0:T(4,128)(2,1)S(1)}, bf16[4,512]{1,0:T(4,128)(2,1)}, u32[]{:S(2)}) copy-start(bf16[4,512]{1,0:T(4,128)(2,1)} %refs_5_.1) | copy-start | bytes 12292
  66.3 129.4 %all-to-all-start.2 = ((bf16[128,64,512]{2,1,0:T(8,128)(2,1)}), bf16[128,64,512]{2,1,0:T(8,128)(2,1)}, u32[]{:S(2)}, u32[]{:S(2)}) async-start(bf16[128,64,512]{2,1,0:T(8,128)(2,1)} %shard_map.106), calls=%async_computation.2 | async-start | bytes 16777216 | tf_op jit(solution)/shard_map/all_to_all | solution.py:337
  138.4 1.5 collective-permute-start.4
  140.8 33.2 %collective-permute-start.5 = (f32[12,512]{1,0:T(8,128)S(1)}, f32[12,512]{1,0:T(8,128)S(1)}, u32[]{:S(2)}, u32[]{:S(2)}) collective-permute-start(f32[12,512]{1,0:T(8,128)S(1)} %pad_maximum_fusion.1), channel_id=1, source_target_pairs={{0,6},{1,7},{2,0},{3,1},{4,2},{5,3},{6,4},{7,5},{8,14},{9,15},{10,... | collective-permute-start | bytes 73736 | tf_op jit(solution)/shard_map/ppermute | solution.py:500
  141.7 32.7 %collective-permute-start.6 = (f32[12,512]{1,0:T(8,128)S(1)}, f32[12,512]{1,0:T(8,128)S(1)}, u32[]{:S(2)}, u32[]{:S(2)}) collective-permute-start(f32[12,512]{1,0:T(8,128)S(1)} %pad_maximum_fusion.1), channel_id=1, source_target_pairs={{0,4},{1,5},{2,6},{3,7},{4,0},{5,1},{6,2},{7,3},{8,12},{9,13},{10,... | collective-permute-start | bytes 73736 | tf_op jit(solution)/shard_map/ppermute | solution.py:500
  142.8 31.5 %collective-permute-start.7 = (f32[12,512]{1,0:T(8,128)S(1)}, f32[12,512]{1,0:T(8,128)S(1)}, u32[]{:S(2)}, u32[]{:S(2)}) collective-permute-start(f32[12,512]{1,0:T(8,128)S(1)} %pad_maximum_fusion.1), channel_id=1, source_target_pairs={{0,2},{1,3},{2,4},{3,5},{4,6},{5,7},{6,0},{7,1},{8,10},{9,11},{10,... | collective-permute-start | bytes 73736 | tf_op jit(solution)/shard_map/ppermute | solution.py:500
  174.5 15.5 %collective-permute-start.10 = (f32[12,512]{1,0:T(8,128)S(1)}, f32[12,512]{1,0:T(8,128)S(1)}, u32[]{:S(2)}, u32[]{:S(2)}) collective-permute-start(f32[12,512]{1,0:T(8,128)S(1)} %pad_maximum_fusion.2), channel_id=1, source_target_pairs={{0,32},{8,40},{16,48},{24,56},{32,64},{40,72},{48,80},{56,88},{64,... | collective-permute-start | bytes 73736 | tf_op jit(solution)/shard_map/ppermute | solution.py:500
  174.5 17.4 %collective-permute-start.8 = (f32[12,512]{1,0:T(8,128)S(1)}, f32[12,512]{1,0:T(8,128)S(1)}, u32[]{:S(2)}, u32[]{:S(2)}) collective-permute-start(f32[12,512]{1,0:T(8,128)S(1)} %pad_maximum_fusion.2), channel_id=1, source_target_pairs={{0,96},{8,104},{16,112},{24,120},{32,0},{40,8},{48,16},{56,24},{64... | collective-permute-start | bytes 73736 | tf_op jit(solution)/shard_map/ppermute | solution.py:500
  176.5 19.0 %collective-permute-start.9 = (f32[12,512]{1,0:T(8,128)S(1)}, f32[12,512]{1,0:T(8,128)S(1)}, u32[]{:S(2)}, u32[]{:S(2)}) collective-permute-start(f32[12,512]{1,0:T(8,128)S(1)} %pad_maximum_fusion.2), channel_id=1, source_target_pairs={{0,64},{8,72},{16,80},{24,88},{32,96},{40,104},{48,112},{56,120},{... | collective-permute-start | bytes 73736 | tf_op jit(solution)/shard_map/ppermute | solution.py:500
  178.3 88.9 %collective-permute-start = (bf16[4,128,512]{2,1,0:T(8,128)(2,1)}, bf16[4,128,512]{2,1,0:T(8,128)(2,1)S(1)}, u32[]{:S(2)}, u32[]{:S(2)}) collective-permute-start(bf16[4,128,512]{2,1,0:T(8,128)(2,1)} %get-tuple-element.23), channel_id=1, source_target_pairs={{0,8},{8,16},{16,24},{24,32},{32,40},{40,48},{48,56},{56,64},{64,7... | collective-permute-start | bytes 1572872 | tf_op jit(solution)/shard_map/ppermute | solution.py:292
  181.3 86.0 %collective-permute-start.1 = (bf16[4,128,512]{2,1,0:T(8,128)(2,1)}, bf16[4,128,512]{2,1,0:T(8,128)(2,1)S(1)}, u32[]{:S(2)}, u32[]{:S(2)}) collective-permute-start(bf16[4,128,512]{2,1,0:T(8,128)(2,1)} %get-tuple-element.24), channel_id=1, source_target_pairs={{8,0},{16,8},{24,16},{32,24},{40,32},{48,40},{56,48},{64,56},{72,6... | collective-permute-start | bytes 1572872 | tf_op jit(solution)/shard_map/ppermute | solution.py:292
  186.4 5.5 %copy-start.9 = (bf16[4,128,512]{2,1,0:T(8,128)(2,1)S(1)}, bf16[4,128,512]{2,1,0:T(8,128)(2,1)}, u32[]{:S(2)}) copy-start(bf16[4,128,512]{2,1,0:T(8,128)(2,1)} %get-tuple-element.26) | copy-start | bytes 1572868
  190.0 77.3 %collective-permute-start.2 = (bf16[4,128,512]{2,1,0:T(8,128)(2,1)S(1)}, bf16[4,128,512]{2,1,0:T(8,128)(2,1)S(1)}, u32[]{:S(2)}, u32[]{:S(2)}) collective-permute-start(bf16[4,128,512]{2,1,0:T(8,128)(2,1)S(1)} %copy-done.10), channel_id=1, source_target_pairs={{0,1},{1,2},{2,3},{3,4},{4,5},{5,6},{6,7},{8,9},{9,10},{10,11},{11... | collective-permute-start | bytes 1572872 | tf_op jit(solution)/shard_map/ppermute | solution.py:292
  191.9 75.3 %collective-permute-start.3 = (bf16[4,128,512]{2,1,0:T(8,128)(2,1)S(1)}, bf16[4,128,512]{2,1,0:T(8,128)(2,1)S(1)}, u32[]{:S(2)}, u32[]{:S(2)}) collective-permute-start(bf16[4,128,512]{2,1,0:T(8,128)(2,1)S(1)} %copy-done.9), channel_id=1, source_target_pairs={{1,0},{2,1},{3,2},{4,3},{5,4},{6,5},{7,6},{9,8},{10,9},{11,10},{12... | collective-permute-start | bytes 1572872 | tf_op jit(solution)/shard_map/ppermute | solution.py:292
  195.7 143.3 %all-to-all-start = ((bf16[128,32,512]{2,1,0:T(8,128)(2,1)}), bf16[128,32,512]{2,1,0:T(8,128)(2,1)}, u32[]{:S(2)}, u32[]{:S(2)}) async-start(bf16[128,32,512]{2,1,0:T(8,128)(2,1)} %shard_map.104), calls=%async_computation | async-start | bytes 8388608 | tf_op jit(solution)/shard_map/all_to_all | solution.py:337
  206.0 58.6 %copy-start.3 = (f32[12,512]{1,0:T(8,128)}, f32[12,512]{1,0:T(8,128)S(1)}, u32[]{:S(2)}) copy-start(f32[12,512]{1,0:T(8,128)S(1)} %pad_maximum_fusion.3.refs_0_) | copy-start | bytes 73732
  206.0 44.8 %collective-permute-start.11 = (f32[12,512]{1,0:T(8,128)S(1)}, f32[12,512]{1,0:T(8,128)S(1)}, u32[]{:S(2)}, u32[]{:S(2)}) collective-permute-start(f32[12,512]{1,0:T(8,128)S(1)} %pad_maximum_fusion.3.refs_0_), channel_id=1, source_target_pairs={{0,8},{8,16},{16,24},{24,0},{32,40},{40,48},{48,56},{56,32},{64,72... | collective-permute-start | bytes 73736 | tf_op jit(solution)/shard_map/ppermute | solution.py:500
  250.9 13.8 %copy-start.4 = (f32[12,512]{1,0:T(8,128)}, f32[12,512]{1,0:T(8,128)S(1)}, u32[]{:S(2)}) copy-start(f32[12,512]{1,0:T(8,128)S(1)} %collective-permute-done.11.refs_1_) | copy-start | bytes 73732
  250.9 6.6 %collective-permute-start.12 = (f32[12,512]{1,0:T(8,128)S(1)}, f32[12,512]{1,0:T(8,128)S(1)}, u32[]{:S(2)}, u32[]{:S(2)}) collective-permute-start(f32[12,512]{1,0:T(8,128)S(1)} %pad_maximum_fusion.3.refs_0_), channel_id=1, source_target_pairs={{0,16},{8,24},{16,0},{24,8},{32,48},{40,56},{48,32},{56,40},{64,80... | collective-permute-start | bytes 73736 | tf_op jit(solution)/shard_map/ppermute | solution.py:500
  257.4 7.2 %copy-start.5 = (f32[12,512]{1,0:T(8,128)}, f32[12,512]{1,0:T(8,128)S(1)}, u32[]{:S(2)}) copy-start(f32[12,512]{1,0:T(8,128)S(1)} %collective-permute-done.12.refs_2_) | copy-start | bytes 73732
  257.4 7.2 %collective-permute-start.13 = (f32[12,512]{1,0:T(8,128)S(1)}, f32[12,512]{1,0:T(8,128)S(1)}, u32[]{:S(2)}, u32[]{:S(2)}) collective-permute-start(f32[12,512]{1,0:T(8,128)S(1)} %pad_maximum_fusion.3.refs_0_), channel_id=1, source_target_pairs={{0,24},{8,0},{16,8},{24,16},{32,56},{40,32},{48,40},{56,48},{64,88... | collective-permute-start | bytes 73736 | tf_op jit(solution)/shard_map/ppermute | solution.py:500
  (4 other events, 10.8 us)
